TPU v7x, 512 devices: a whole 4x8x8 slice. The times are simulated.
512 devices in a mesh: grp: 16 (over y, x_lo), blk: 32 (over z, x_hi, core).
Axes of the slice: x: 4 (x_hi: 2, x_lo: 2; x = x_hi * 2 + x_lo), y: 8, z: 8, core: 2. Of those that a mesh axis runs over, the one named last changes fastest.
Arguments:
- amplitudes: float32 [128, 128, 2048], P('blk', None, 'grp'), may hold values from -6 to 6
- ladder_ints: float32 [2048, 2048], P('grp', 'blk'), may hold values from -0.375 to 0.375
- cycle_ints: float32 [2048, 2048], P('grp', 'blk'), may hold values from -0.375 to 0.375
- occ_coupling: float32 [128, 128], replicated, may hold values from -1.5 to 1.5
- occ_irrep: int32 [128], replicated, may hold values from 0 to 7
- pair_irrep: int32 [16], replicated, may hold values from 0 to 7
- screen: int32 [16, 16], replicated, may hold values 0 or 1
- block_order: int32 [16], replicated, may hold values from 0 to 15, each once
Outputs:
- residual: float32 [128, 128, 2048], P('blk', None, 'grp')
Inputs may be any that keep to these rules, and one draw needn't show every extreme that they name: block_order names every block once.
All inputs are finite; a program needn't handle non-finite values.
Results may differ from a plain program's by a relative error of at most 0.000071.
Values sent between devices are 32-bit elements; how exact they have to be, the bound alone decides.
A program may use at most 64 MiB of HBM per device.

v0:
```python
import jax
import jax.numpy as jnp
from jax import lax
from jax.sharding import PartitionSpec as P


def shards(
    amplitudes, ladder_ints, cycle_ints, occ_coupling, occ_irrep, pair_irrep, screen, block_order
):
    highest = lax.Precision.HIGHEST
    rows_i, occ, cols_g = amplitudes.shape
    nblocks = pair_irrep.shape[0]
    blk_grp = nblocks // lax.axis_size("grp")
    tile = cols_g // blk_grp
    grp_id = lax.axis_index("grp")
    row_id = lax.axis_index("blk")
    my_occ = lax.dynamic_slice_in_dim(occ_irrep, row_id * rows_i, rows_i)
    my_labels = lax.dynamic_slice_in_dim(pair_irrep, grp_id * blk_grp, blk_grp)
    my_screen = lax.dynamic_slice_in_dim(screen, grp_id * blk_grp, blk_grp, 0).astype(jnp.float32)
    pair_sym = jnp.bitwise_xor(my_occ[:, None], occ_irrep[None, :])
    amp_mask = (pair_sym[:, :, None] == my_labels[None, None, :]).astype(jnp.float32)
    amps3 = (amplitudes.reshape(rows_i, occ, blk_grp, tile) * amp_mask[:, :, :, None]).reshape(
        rows_i, occ, cols_g
    )
    amps = amps3.reshape(rows_i * occ, cols_g)
    coupling = occ_coupling * (occ_irrep[:, None] == occ_irrep[None, :]).astype(jnp.float32)
    label_cols = pair_irrep.astype(jnp.float32)[None, :]
    mine_rows = my_labels.astype(jnp.float32)[:, None]
    local_panels = jnp.stack((ladder_ints, cycle_ints))
    piece = lax.all_gather(local_panels, "blk", axis=2, tiled=True)
    count = piece.shape[2]
    col_blk = jnp.arange(count, dtype=jnp.int32) // tile
    onehot = (col_blk[None, :] == jnp.arange(nblocks, dtype=jnp.int32)[:, None]).astype(jnp.float32)
    col_lab = jnp.dot(label_cols, onehot, precision=highest)
    same = (mine_rows == col_lab).astype(jnp.float32)
    kept = jnp.dot(my_screen, onehot, precision=highest)
    keep_ladder = same * kept
    ladder_panel = (piece[0].reshape(blk_grp, tile, count) * keep_ladder[:, None, :]).reshape(
        cols_g, count
    )
    cycle_panel = (piece[1].reshape(blk_grp, tile, count) * same[:, None, :]).reshape(cols_g, count)
    ladder = jnp.dot(amps, ladder_panel, precision=highest, preferred_element_type=jnp.float32)
    inner = jnp.dot(amps, cycle_panel, precision=highest, preferred_element_type=jnp.float32)
    cycle = jnp.einsum(
        "ikx,kj->ijx", inner.reshape(rows_i, occ, count), coupling, precision=highest
    )
    partial_value = ladder + cycle.reshape(rows_i * occ, count)
    ordered = jnp.take(partial_value.reshape(rows_i, occ, nblocks, tile), block_order, axis=2)
    ordered = ordered.reshape(rows_i, occ, nblocks * tile)
    moved = lax.all_to_all(ordered, "blk", split_axis=1, concat_axis=0, tiled=True)
    anti = ordered - jnp.transpose(moved, (1, 0, 2))
    result = lax.psum_scatter(anti, "grp", scatter_dimension=2, tiled=True)
    return result


def solution(mesh):
    placed = (P("blk", None, "grp"), P("grp", "blk"), P("grp", "blk"), P(), P(), P(), P(), P())
    return jax.shard_map(
        shards, mesh=mesh, in_specs=placed, out_specs=P("blk", None, "grp"), check_vma=False
    )
```

profile of v0, /device:TPU:1, one launch (start us, length us, event | category | flops | bytes accessed | tf_op | source)
XLA Modules:
  0.0 361.4 jit_solution(6302833797781969086)
XLA Ops:
  6.5 0.0 copy-start.2
  6.5 0.0 copy-start.1
  6.5 0.0 all-gather.2.cloned.1.call-start
  6.5 1.4 pad_maximum_fusion
  8.0 0.0 all-gather.2.cloned.1.call-update
  8.0 0.0 reduce-scatter.2.cloned.1.call-start
  8.1 1.3 dynamic_slice.10
  10.1 0.9 fusion.8
  10.9 0.8 fusion.9
  11.8 0.7 dynamic_slice.9
  12.5 0.7 compare_select_fusion
  13.2 0.7 compare_and_fusion
  13.9 0.1 broadcast_bitcast_fusion
  13.9 1.4 fusion.22
  15.3 1.1 broadcast_multiply_fusion
  16.4 86.4 %all-gather.2.cloned.1.call-done = f32[2,128,2048]{1,2,0:T(8,128)} async-done(((f32[2,128,64]{1,2,0:T(8,128)}), f32[2,128,2048]{1,2,0:T(8,128)}) %all-gather.2.cloned.1.call-update) | async-done | bytes 2097168 | tf_op jit(solution)/shard_map/all_gather | solution.py:30
  102.8 4.8 %fusion.2 = f32[4,128,2048]{2,1,0:T(8,128)S(1)} fusion(f32[4,128,128]{2,1,0:T(8,128)S(1)} %broadcast_multiply_fusion, f32[2,128,2048]{1,2,0:T(8,128)} %all-gather.2.cloned.1.call-done, f32[2048]{0:T(1024)S(1)} %convert_element_type.28), kind=kOutput, calls=%fused_computation.7 | convolution fusion | flops 1610874880 | bytes 5513216 | tf_op jit(solution)/shard_map/dot_general | solution.py:43
  107.6 0.0 copy-done.2
  107.6 0.0 copy-done.1
  107.6 0.0 copy-start
  107.7 4.1 %fusion.10 = f32[128,4,2048]{2,0,1:T(8,128)S(1)} fusion(f32[4,128,2048]{2,1,0:T(8,128)S(1)} %fusion.2, f32[128,128]{1,0:T(8,128)S(1)} %copy-done.1, s32[128]{0:T(128)S(1)} %copy-done.2), kind=kOutput, calls=%fused_computation.17 | convolution fusion | flops 1610645504 | bytes 8454656 | tf_op jit(solution)/shard_map/ikx,kj->ijx/dot_general | solution.py:44
  111.8 0.0 copy-done
  111.8 3.6 %fusion = f32[64,8,16,128]{3,1,2,0:T(8,128)S(1)} fusion(f32[128,4,2048]{2,0,1:T(8,128)S(1)} %fusion.10, f32[512,128]{1,0:T(8,128)S(1)} %bitcast.55, f32[2,128,2048]{1,2,0:T(8,128)S(1)} %copy-done, f32[2048]{0:T(1024)S(1)} %get-tuple-element.5), kind=kOutput, calls=%fused_computation.4 | convolution fusion | flops 1611923456 | bytes 9707520 | tf_op jit(solution)/shard_map/dot_general | solution.py:42
  115.4 1.1 copy.40
  116.5 3.2 copy.30
  119.7 5.0 %gather_fusion = f32[16,4,128,128]{3,2,1,0:T(8,128)} fusion(f32[4,128,16,128]{3,1,2,0:T(8,128)} %copy.30, s32[1024]{0:T(1024)S(1)} %pad_clamp_fusion), kind=kCustom, calls=%fused_computation | custom fusion | bytes 8388672 | tf_op jit(solution)/shard_map/jit(_take)/gather | solution.py:48
  124.7 5.3 %copy.31 = f32[4,128,16,128]{1,3,2,0:T(8,128)} copy(f32[4,128,16,128]{3,1,0,2:T(8,128)} %bitcast.51) | data formatting | bytes 8388608 | tf_op jit(solution)/shard_map/jit(_take)/gather | solution.py:48
  130.1 3.8 %bitcast_select_fusion = f32[4,128,2048]{1,2,0:T(8,128)} fusion(f32[4,128,16,128]{1,3,2,0:T(8,128)} %copy.31, pred[2048]{0:T(1024)(128)(4,1)S(1)} %broadcast_bitcast_fusion), kind=kLoop, calls=%fused_computation.3 | loop fusion | flops 1048576 | bytes 8390656 | tf_op jit(solution)/shard_map/jit(_take)/select_n | solution.py:48
  133.9 5.5 %copy.32 = f32[4,128,2048]{2,0,1:T(4,128)} copy(f32[4,128,2048]{1,2,0:T(8,128)} %bitcast_select_fusion) | data formatting | bytes 8388608 | tf_op jit(solution)/shard_map/jit(_take)/select_n | solution.py:48
  139.3 100.1 %all_to_all.18 = f32[4,128,2048]{2,0,1:T(4,128)S(1)} all-to-all(f32[4,128,2048]{2,0,1:T(4,128)} %copy.32), channel_id=1, replica_groups=mesh['grp'=16,'blk'=32] {'blk'}, dimensions={1} | all-to-all | bytes 8388608 | tf_op jit(solution)/shard_map/all_to_all | solution.py:50
  239.4 5.5 %copy.33 = f32[32,4,4,2048]{3,2,1,0:T(4,128)} copy(f32[32,4,4,2048]{3,1,2,0:T(4,128)S(1)} %bitcast.53) | data formatting | bytes 8388608 | tf_op jit(solution)/shard_map/all_to_all | solution.py:50
  245.0 5.3 %copy.34 = f32[128,4,2048]{0,2,1:T(8,128)} copy(f32[128,4,2048]{2,1,0:T(4,128)} %bitcast.54) | data formatting | bytes 8388608 | tf_op jit(solution)/shard_map/all_to_all | solution.py:50
  250.3 5.1 %bitcast_subtract_fusion = f32[4,128,2048]{1,2,0:T(8,128)} fusion(f32[128,4,2048]{0,2,1:T(8,128)} %copy.34, f32[4,128,16,128]{1,3,2,0:T(8,128)} %copy.31, pred[2048]{0:T(1024)(128)(4,1)S(1)} %broadcast_bitcast_fusion), kind=kLoop, calls=%fused_computation.2 | loop fusion | flops 2097152 | bytes 12584960 | tf_op jit(solution)/shard_map/sub | solution.py:51
  255.3 0.0 reduce-scatter.2.cloned.1.call-update
  255.3 97.4 %reduce-scatter.2.cloned.1.call-done = f32[4,128,128]{1,2,0:T(8,128)} async-done(((f32[4,128,2048]{1,2,0:T(8,128)}), f32[4,128,128]{1,2,0:T(8,128)}) %reduce-scatter.2.cloned.1.call-update) | async-done | bytes 262160 | tf_op jit(solution)/shard_map/reduce_scatter | solution.py:52
  352.7 1.8 copy.35
  (4 shorter events, 0.0 us)
Async XLA Ops:
  6.5 101.1 %copy-start.2 = (s32[128]{0:T(128)S(1)}, s32[128]{0:T(128)}, u32[]{:S(2)}) copy-start(s32[128]{0:T(128)} %param.12) | copy-start | bytes 1540
  6.5 101.1 %copy-start.1 = (f32[128,128]{1,0:T(8,128)S(1)}, f32[128,128]{1,0:T(8,128)}, u32[]{:S(2)}) copy-start(f32[128,128]{1,0:T(8,128)} %param.11) | copy-start | bytes 196612
  6.5 96.2 %all-gather.2.cloned.1.call-start = ((), (), s32[]{:S(2)}) async-start(), calls=%async_computation.2 | async-start | bytes 2162688 | tf_op jit(solution)/shard_map/all_gather | solution.py:30
  8.0 344.7 %reduce-scatter.2.cloned.1.call-start = ((), (), s32[]{:S(2)}) async-start(), calls=%async_computation.3 | async-start | bytes 4456448 | tf_op jit(solution)/shard_map/reduce_scatter | solution.py:52
  107.6 4.1 %copy-start = (f32[2,128,2048]{1,2,0:T(8,128)S(1)}, f32[2,128,2048]{1,2,0:T(8,128)}, u32[]{:S(2)}) copy-start(f32[2,128,2048]{1,2,0:T(8,128)} %all-gather.2.cloned.1.call-done) | copy-start | bytes 6291460
Sparse Core Ops, SparseCore 0:
  10.8 91.9 all-gather.1
  255.5 97.2 reduce-scatter.1
where the time goes:
time: 364 us; the launch traced here: 361 us
  waiting for transfers between devices  184 us (51%)
  blocking collectives  100 us (27%)
  local copies, waits for them, and re-layouts  34.9 us (10%)
  matrix products  14.2 us (4%)
  between operations  14.2 us (4%)
  other arithmetic  14.1 us (4%)
    all_to_all x1, blocking collectives, shards(): lax.all_to_all(ordered, 'blk', split_axis=1, concat_axis=0, tiled=True)  100 us
    reduce_scatter x1, waiting for transfers between devices, shards(): result = lax.psum_scatter(anti, 'grp', scatter_dimension=2, tiled=True)  97.4 us
    all_gather x1, waiting for transfers between devices, shards(): piece = lax.all_gather(local_panels, 'blk', axis=2, tiled=True)  86.4 us
    all_to_all x2, local copies, waits for them, and re-layouts, shards(): lax.all_to_all(ordered, 'blk', split_axis=1, concat_axis=0, tiled=True)  10.8 us
    gather x2, local copies, waits for them, and re-layouts, shards(): jnp.take(partial_value.reshape(rows_i, occ, nblocks, tile), block_order,...  10.3 us
  transfers between devices with their start and end apart: 2, of which 2 were waited for; matrix products, arithmetic and copies ran while one was open for 2% of the time, Pallas kernels for 0%

commit v1 on v0

v1 whole, which is shorter than its diff:
```python
import functools

import jax
import jax.numpy as jnp
from jax import lax
from jax.experimental import pallas as pl
from jax.experimental.pallas import tpu as pltpu
from jax.sharding import PartitionSpec as P

CAP = 32
ROWS = 4
TILE = 128
HIGH = lax.Precision.HIGHEST
NT = (((1,), (1,)), ((), ()))


def split(x):
    hi = x.astype(jnp.bfloat16)
    return hi, (x - hi.astype(jnp.float32)).astype(jnp.bfloat16)


def kernel(
    nz, ny,
    round_s, irr_s, pair_s, screen_s, order_s, irr_v, coup, amps, lad, cyc,
    out, count_s,
    psub, pan, lhs, lhs_hi, lhs_lo, part, xs, xb, ys, yb, res4, full, own, send, back,
    sem_a, sem_b, sem_c, sem_x, sem_y, sem_f, sem_h,
):
    nblk = 4 * nz
    occ = amps.shape[1]
    slots = ROWS * CAP
    g = lax.axis_index("grp")
    b = lax.axis_index("blk")
    z = lax.div(b, 4)
    plane = lax.rem(b, 4)
    h = lax.div(plane, 2)
    c = lax.rem(plane, 2)
    y = lax.div(g, 2)
    xl = lax.rem(g, 2)
    x_dev = z * 4 + (1 - h) * 2 + c
    c_dev = z * 4 + h * 2 + (1 - c)
    x_plane = (1 - h) * 2 + c

    barrier = pltpu.get_barrier_semaphore()

    def greet_blk(d, carry):
        pl.semaphore_signal(
            barrier, inc=1, device_id={"blk": lax.rem(b + d, nblk)}, device_id_type=pl.DeviceIdType.MESH
        )
        return carry

    lax.fori_loop(1, nblk, greet_blk, 0)

    def greet_grp(d, carry):
        pl.semaphore_signal(
            barrier, inc=1, device_id={"grp": lax.rem(y + d, ny) * 2 + xl}, device_id_type=pl.DeviceIdType.MESH
        )
        return carry

    lax.fori_loop(1, ny, greet_grp, 0)
    pl.semaphore_signal(
        barrier, inc=1, device_id={"grp": y * 2 + 1 - xl}, device_id_type=pl.DeviceIdType.MESH
    )

    my_label = pair_s[g]
    tile_id = lax.div(b, 2)
    same = jnp.where(pair_s[tile_id] == my_label, 1.0, 0.0)
    kept = same * screen_s[g, tile_id].astype(jnp.float32)
    lad_t = lad[...].T * kept
    cyc_t = cyc[...].T * same
    for s in range(2):
        psub[s, :, 0:TILE] = lad_t[32 * s : 32 * s + 32]
        psub[s, :, TILE : 2 * TILE] = cyc_t[32 * s : 32 * s + 32]
    pan[z, h] = psub[h]

    irr_b = jnp.broadcast_to(irr_v[...].astype(jnp.float32), (occ, occ))
    irr_t = irr_b.T
    equal = irr_b == irr_t
    before = lax.broadcasted_iota(jnp.int32, (occ, occ), 0) < lax.broadcasted_iota(
        jnp.int32, (occ, occ), 1
    )
    rank = jnp.sum(jnp.where(equal & before, 1.0, 0.0), axis=0, keepdims=True)
    key = irr_v[...].astype(jnp.float32) * occ + rank
    count_s[0] = jnp.max(rank).astype(jnp.int32) + 1

    def targets(label, place):
        goal = place.astype(jnp.float32)
        for i in reversed(range(ROWS)):
            base = (irr_s[b * ROWS + i] ^ label) * occ + round_s[0] * CAP - CAP * i
            at = place.astype(jnp.float32) + base.astype(jnp.float32)
            goal = at if i == ROWS - 1 else jnp.where(place < CAP * (i + 1), at, goal)
        return goal

    key_b = jnp.broadcast_to(key, (slots, occ))
    sel = jnp.where(
        key_b == targets(my_label, lax.broadcasted_iota(jnp.int32, (slots, occ), 0)), 1.0, 0.0
    )
    coupling = jnp.where(equal, coup[...], 0.0)
    sel_c = lax.dot_general(sel, coupling, NT, precision=HIGH, preferred_element_type=jnp.float32)
    for i in range(ROWS):
        rows = slice(CAP * i, CAP * i + CAP)
        pick = jnp.concatenate((sel[rows], sel_c[rows]), axis=0)
        packed = jnp.dot(pick, amps[i], precision=HIGH, preferred_element_type=jnp.float32)
        lhs[plane, rows, 0:TILE] = packed[:CAP]
        lhs[plane, rows, TILE : 2 * TILE] = packed[CAP:]

    pl.semaphore_wait(barrier, nblk - 1 + ny)

    def remote(src, dst, sems, index, where):
        return pltpu.make_async_remote_copy(
            src_ref=src,
            dst_ref=dst,
            send_sem=sems.at[(0, *index)],
            recv_sem=sems.at[(1, *index)],
            device_id=where,
            device_id_type=pl.DeviceIdType.MESH,
        )

    def to_x():
        return remote(psub.at[1 - h], pan.at[z, h], sem_b, (0,), {"blk": x_dev})

    def from_x():
        return remote(psub.at[1 - h], pan.at[z, 1 - h], sem_b, (0,), {"blk": x_dev})

    def along_z(which, k, d):
        return remote(
            pan.at[z, which], pan.at[z, which], sem_c, (k, d), {"blk": lax.rem(z + d, nz) * 4 + plane}
        )

    def rows_to(src, where, k):
        return remote(lhs.at[src], lhs.at[src], sem_a, (k,), {"blk": where})

    to_x().start()
    rows_to(plane, x_dev, 0).start()

    def start_own(d, carry):
        along_z(h, 0, d).start()
        return carry

    lax.fori_loop(1, nz, start_own, 0)
    rows_to(plane, c_dev, 1).start()
    from_x().wait_recv()

    def start_other(d, carry):
        along_z(1 - h, 1, d).start()
        return carry

    lax.fori_loop(1, nz, start_other, 0)
    rows_to(x_plane, x_dev, 0).wait_recv()
    rows_to(x_plane, c_dev, 2).start()
    rows_to(h * 2 + 1 - c, c_dev, 1).wait_recv()
    rows_to((1 - h) * 2 + 1 - c, c_dev, 2).wait_recv()
    hi, lo = split(lhs[...].reshape(4 * slots, 2 * TILE))
    lhs_hi[...] = hi
    lhs_lo[...] = lo

    def multiply(src):
        hi, lo = split(pan[src].reshape(64, 2 * TILE))
        value = lax.dot_general(hi, lhs_hi[...], NT, preferred_element_type=jnp.float32)
        value += lax.dot_general(hi, lhs_lo[...], NT, preferred_element_type=jnp.float32)
        value += lax.dot_general(lo, lhs_hi[...], NT, preferred_element_type=jnp.float32)
        part[src * 2] = value[:32]
        part[src * 2 + 1] = value[32:]

    multiply(z)

    def take_z(d, carry):
        src = lax.rem(z + nz - d, nz)
        remote(pan.at[z, h], pan.at[src, h], sem_c, (0, d), {"blk": x_dev}).wait_recv()
        remote(pan.at[z, h], pan.at[src, 1 - h], sem_c, (1, d), {"blk": x_dev}).wait_recv()
        multiply(src)
        return carry

    lax.fori_loop(1, nz, take_z, 0)

    def pair_copy(k):
        return remote(xs.at[k], xb.at[k], sem_x, (k,), {"grp": y * 2 + 1 - xl})

    def y_copy(k):
        return remote(ys.at[k], yb.at[k], sem_y, (k,), {"grp": lax.rem(y + k, ny) * 2 + xl})

    def send_x(n, carry):
        k = lax.rem(n + 1, ny)
        xs[k] = part[order_s[lax.rem(y + k, ny) * 2 + 1 - xl]]
        pair_copy(k).start()
        return carry

    lax.fori_loop(0, ny, send_x, 0)

    def send_y(k, carry):
        pair_copy(k).wait_recv()
        ys[k] = part[order_s[lax.rem(y + k, ny) * 2 + xl]] + xb[k]
        y_copy(k).start()
        return carry

    lax.fori_loop(1, ny, send_y, 0)
    pair_copy(0).wait_recv()
    total = part[order_s[g]] + xb[0]

    def take_y(k, total):
        y_copy(k).wait_recv()
        return total + yb[k]

    total = lax.fori_loop(1, ny, take_y, total)

    quarter = c * 2 + h
    for r in range(4):
        res4[r] = total[:, slots * r : slots * (r + 1)]

    def plane_copy(d):
        to = lax.rem(plane + d, 4)
        return remote(res4.at[to], full.at[quarter], sem_f, (d,), {"blk": z * 4 + to})

    for d in range(1, 4):
        plane_copy(d).start()
    full[quarter] = res4[plane]

    out_label = pair_s[order_s[g]]
    key_t = jnp.broadcast_to(key, (slots, occ)).T
    lane = lax.broadcasted_iota(jnp.int32, (occ, slots), 1)
    place = jnp.where(key_t == targets(out_label, lane), 1.0, 0.0)
    for d in range(1, 4):
        other = lax.rem(plane + 4 - d, 4)
        other_quarter = lax.rem(other, 2) * 2 + lax.div(other, 2)
        remote(res4.at[0], full.at[other_quarter], sem_f, (d,), {"blk": c_dev}).wait_recv()
    full_t = full[...].reshape(TILE, slots).T
    for i in range(ROWS):
        mine = (lane >= CAP * i) & (lane < CAP * (i + 1))
        value = jnp.dot(
            jnp.where(mine, place, 0.0), full_t, precision=HIGH, preferred_element_type=jnp.float32
        )
        own[i] = value
        send[pl.ds(i, occ, stride=ROWS), :] = value

    def swap(d):
        to = lax.rem(b + d, nblk)
        return remote(
            send.at[pl.ds(pl.multiple_of(to * 16, 16), 16)],
            back.at[pl.ds(pl.multiple_of(b * 16, 16), 16)],
            sem_h,
            (d,),
            {"blk": to},
        )

    def start_swap(d, carry):
        swap(d).start()
        return carry

    lax.fori_loop(1, nblk, start_swap, 0)
    here = pl.ds(pl.multiple_of(b * 16, 16), 16)
    back[here] = send[here]

    def take_swap(d, carry):
        src = lax.rem(b + nblk - d, nblk)
        remote(
            send.at[here], back.at[pl.ds(pl.multiple_of(src * 16, 16), 16)], sem_h, (d,), {"blk": c_dev}
        ).wait_recv()
        return carry

    lax.fori_loop(1, nblk, take_swap, 0)
    for j in range(ROWS):
        for i in range(ROWS):
            at = pl.ds(i, nblk, stride=ROWS)
            out[j, at, :] = own[j, at, :] - back[pl.ds(ROWS * j + i, nblk, stride=16), :]

    to_x().wait_send()
    rows_to(plane, x_dev, 0).wait_send()
    rows_to(plane, c_dev, 1).wait_send()
    rows_to(x_plane, c_dev, 2).wait_send()

    def end_z(d, carry):
        along_z(h, 0, d).wait_send()
        along_z(1 - h, 1, d).wait_send()
        return carry

    lax.fori_loop(1, nz, end_z, 0)
    pair_copy(0).wait_send()

    def end_y(k, carry):
        pair_copy(k).wait_send()
        y_copy(k).wait_send()
        return carry

    lax.fori_loop(1, ny, end_y, 0)
    for d in range(1, 4):
        plane_copy(d).wait_send()

    def end_swap(d, carry):
        swap(d).wait_send()
        return carry

    lax.fori_loop(1, nblk, end_swap, 0)


def shards(
    amplitudes, ladder_ints, cycle_ints, occ_coupling, occ_irrep, pair_irrep, screen, block_order
):
    rows, occ, tile = amplitudes.shape
    nz = lax.axis_size("blk") // 4
    ny = lax.axis_size("grp") // 2
    slots = ROWS * CAP
    f32 = jnp.float32
    smem = pl.BlockSpec(memory_space=pltpu.SMEM)
    vmem = pl.BlockSpec(memory_space=pltpu.VMEM)
    dma = pltpu.SemaphoreType.DMA
    call = pl.pallas_call(
        functools.partial(kernel, nz, ny),
        out_shape=(
            jax.ShapeDtypeStruct((rows, occ, tile), f32),
            jax.ShapeDtypeStruct((1,), jnp.int32),
        ),
        in_specs=[smem] * 5 + [vmem] * 5,
        out_specs=(vmem, smem),
        scratch_shapes=[
            pltpu.VMEM((2, 32, 2 * TILE), f32),
            pltpu.VMEM((nz, 2, 32, 2 * TILE), f32),
            pltpu.VMEM((4, slots, 2 * TILE), f32),
            pltpu.VMEM((4 * slots, 2 * TILE), jnp.bfloat16),
            pltpu.VMEM((4 * slots, 2 * TILE), jnp.bfloat16),
            pltpu.VMEM((2 * nz, 32, 4 * slots), f32),
            pltpu.VMEM((ny, 32, 4 * slots), f32),
            pltpu.VMEM((ny, 32, 4 * slots), f32),
            pltpu.VMEM((ny, 32, 4 * slots), f32),
            pltpu.VMEM((ny, 32, 4 * slots), f32),
            pltpu.VMEM((4, 32, slots), f32),
            pltpu.VMEM((4, 32, slots), f32),
            pltpu.VMEM((rows, occ, tile), f32),
            pltpu.VMEM((rows * occ, tile), f32),
            pltpu.VMEM((rows * occ, tile), f32),
            dma((2, 3)),
            dma((2, 1)),
            dma((2, 2, nz)),
            dma((2, ny)),
            dma((2, ny)),
            dma((2, 4)),
            dma((2, 4 * nz)),
        ],
        compiler_params=pltpu.CompilerParams(
            collective_id=0, has_side_effects=True, vmem_limit_bytes=24 << 20
        ),
    )

    def part(index):
        return call(
            jnp.full((1,), index, jnp.int32),
            occ_irrep, pair_irrep, screen, block_order, occ_irrep.reshape(1, occ),
            occ_coupling, amplitudes, ladder_ints, cycle_ints,
        )

    first, count = part(0)
    rounds = (count[0] + CAP - 1) // CAP

    def more(state):
        return state[0] < rounds

    def again(state):
        return state[0] + 1, state[1] + part(state[0])[0]

    return lax.while_loop(more, again, (jnp.int32(1), first))[1]


def solution(mesh):
    placed = (P("blk", None, "grp"), P("grp", "blk"), P("grp", "blk"), P(), P(), P(), P(), P())
    return jax.shard_map(
        shards, mesh=mesh, in_specs=placed, out_specs=P("blk", None, "grp"), check_vma=False
    )
```

time: 364 us -> 69.6 us (0.19)
  waiting for transfers between devices: 184 us -> 0 us
  blocking collectives: 100 us -> 0 us
  Pallas kernels: 0 us -> 66.3 us
  local copies, waits for them, and re-layouts: 34.9 us -> 2.38 us
  matrix products: 14.2 us -> 0 us
  other arithmetic: 14.1 us -> 0 us
  between operations: 14.2 us -> 0.74 us
    all_to_all x1 -> x0, blocking collectives: 100 us -> none  [shards(): lax.all_to_all(ordered, 'blk', split_axis=1, concat_axis=0, tiled=True)]
    reduce_scatter x1 -> x0, waiting for transfers between devices: 97.4 us -> none  [shards(): result = lax.psum_scatter(anti, 'grp', scatter_dimension=2, tiled=True)]
    all_gather x1 -> x0, waiting for transfers between devices: 86.4 us -> none  [shards(): piece = lax.all_gather(local_panels, 'blk', axis=2, tiled=True)]
    pallas_call x0 -> x1, Pallas kernels: none -> 66.3 us  [part(): call(jnp.full((1,), index, jnp.int32), occ_irrep, pair_irrep, screen, blo...]
    dot_general x5 -> x0, matrix products: 14.2 us -> none  [the longest x1 4.82 us: shards(): jnp.dot(amps, cycle_panel, precision=highest, preferred_element_type=jnp....]
    all_to_all x2 -> x0, local copies, waits for them, and re-layouts: 10.8 us -> none  [shards(): lax.all_to_all(ordered, 'blk', split_axis=1, concat_axis=0, tiled=True)]
    gather x2 -> x0, local copies, waits for them, and re-layouts: 10.3 us -> none  [shards(): jnp.take(partial_value.reshape(rows_i, occ, nblocks, tile), block_order,...]
    select_n x1 -> x0, local copies, waits for them, and re-layouts: 5.48 us -> none  [shards(): jnp.take(partial_value.reshape(rows_i, occ, nblocks, tile), block_order,...]
  transfers between devices with their start and end apart: 2 -> 0, of which waited for: 2 -> 0; matrix products, arithmetic and copies ran while one was open for 2% -> 0% of each run, Pallas kernels for 0% -> 0%
where the time goes in v1:
time: 69.6 us; the launch traced here: 69.4 us
  Pallas kernels  66.3 us (95%)
  local copies, waits for them, and re-layouts  2.38 us (3%)
  between operations  0.74 us (1%)
    pallas_call x1, Pallas kernels, part(): call(jnp.full((1,), index, jnp.int32), occ_irrep, pair_irrep, screen, blo...  66.3 us
    unnamed x17, local copies, waits for them, and re-layouts  2.38 us

profile of v1, /device:TPU:1, one launch (start us, length us, event | category | flops | bytes accessed | tf_op | source)
XLA Modules:
  0.0 69.4 jit_solution(3769400326532727653)
XLA Ops:
  0.0 0.0 copy-start.4
  0.0 0.9 %copy.9.lad = f32[128,64]{1,0:T(8,128)S(1)} copy(f32[128,64]{0,1:T(8,128)} %param.11) | data formatting | bytes 65536 | tf_op args[1]
  0.9 0.0 copy-done.4
  0.9 0.0 copy-start.1
  0.9 0.0 copy-start.2
  0.9 0.0 copy-start.3
  0.9 0.0 copy-start.5
  0.9 0.0 copy-start.6
  0.9 0.1 copy.10.cyc
  1.0 0.7 copy-done.1
  1.7 0.0 copy-done.2
  1.7 0.0 copy-done.3
  1.7 0.0 copy-done.5
  1.7 0.0 copy-done.6
  1.7 0.0 copy-start
  1.7 66.3 %shard_map.82 = (f32[4,128,128]{2,1,0:T(8,128)S(1)}, s32[1]{0:T(128)}) custom-call(s32[1]{0:T(128)} %constant.19.clone.1.round_s, s32[128]{0:T(128)S(1)} %copy-done.3, s32[16]{0:T(128)S(1)} %copy-done.5, s32[16,16]{1,0:T(8,128)S(1)} %copy-done.2, s32[16]{0:T(128)S(1)} %copy-done.6, s32[1,128]{1,0:T(1,128)S(1)} %bitcast.8, f32[128,128]{1,0:T(8,128)S(1)} %copy-done.1, ...), custom_call_target="tpu_custom_call" | custom-call | tf_op jit(solution)/shard_map/pallas_call | solution.py:344
  68.7 0.0 copy-done
  68.7 0.7 %copy.20 = f32[4,128,128]{2,1,0:T(8,128)} copy(f32[4,128,128]{2,1,0:T(8,128)S(1)} %get-tuple-element.68) | data formatting | bytes 524288
  (1 shorter events, 0.0 us)
Async XLA Ops:
  0.0 0.9 %copy-start.4 = (f32[128,64]{0,1:T(8,128)S(1)}, f32[128,64]{0,1:T(8,128)}, u32[]{:S(2)}) copy-start(f32[128,64]{0,1:T(8,128)} %param.12) | copy-start | bytes 98308
  0.9 0.8 %copy-start.1 = (f32[128,128]{1,0:T(8,128)S(1)}, f32[128,128]{1,0:T(8,128)}, u32[]{:S(2)}) copy-start(f32[128,128]{1,0:T(8,128)} %coup.1) | copy-start | bytes 196612
  0.9 0.8 %copy-start.2 = (s32[16,16]{1,0:T(8,128)S(1)}, s32[16,16]{1,0:T(8,128)}, u32[]{:S(2)}) copy-start(s32[16,16]{1,0:T(8,128)} %screen_s.1) | copy-start | bytes 3076
  0.9 0.8 %copy-start.3 = (s32[128]{0:T(128)S(1)}, s32[128]{0:T(128)}, u32[]{:S(2)}) copy-start(s32[128]{0:T(128)} %irr_s.1) | copy-start | bytes 1540
  0.9 0.8 %copy-start.5 = (s32[16]{0:T(128)S(1)}, s32[16]{0:T(128)}, u32[]{:S(2)}) copy-start(s32[16]{0:T(128)} %pair_s.1) | copy-start | bytes 196
  0.9 0.8 %copy-start.6 = (s32[16]{0:T(128)S(1)}, s32[16]{0:T(128)}, u32[]{:S(2)}) copy-start(s32[16]{0:T(128)} %order_s.1) | copy-start | bytes 196
  1.7 66.9 %copy-start = (f32[4,128,128]{2,1,0:T(8,128)S(1)}, f32[4,128,128]{2,1,0:T(8,128)}, u32[]{:S(2)}) copy-start(f32[4,128,128]{2,1,0:T(8,128)} %amps.1) | copy-start | bytes 786436

commit v2 on v1

--- a/solution.py
+++ b/solution.py
@@ -8,6 +8,7 @@
 from jax.sharding import PartitionSpec as P
 
 CAP = 32
+JOINT = 384
 ROWS = 4
 TILE = 128
 HIGH = lax.Precision.HIGHEST
@@ -21,11 +22,14 @@
 
 def kernel(
     nz, ny,
-    round_s, irr_s, pair_s, screen_s, order_s, irr_v, coup, amps, lad, cyc,
-    out, count_s,
-    psub, pan, lhs, lhs_hi, lhs_lo, part, xs, xb, ys, yb, res4, full, own, send, back,
-    sem_a, sem_b, sem_c, sem_x, sem_y, sem_f, sem_h,
+    *refs,
 ):
+    given, (out, count_s), held = refs[:10], refs[10:12], refs[12:22]
+    round_s, irr_s, pair_s, screen_s, order_s, irr_v, coup, amps, lad, cyc = held
+    (
+        psub, pan, lhs, lhs_hi, lhs_lo, pack, part, xs, xb, ys, yb, res4, full, own, send, back,
+        sem_in, sem_a, sem_b, sem_c, sem_x, sem_y, sem_f, sem_h,
+    ) = refs[22:]
     nblk = 4 * nz
     occ = amps.shape[1]
     slots = ROWS * CAP
@@ -43,31 +47,39 @@
 
     barrier = pltpu.get_barrier_semaphore()
 
-    def greet_blk(d, carry):
-        pl.semaphore_signal(
-            barrier, inc=1, device_id={"blk": lax.rem(b + d, nblk)}, device_id_type=pl.DeviceIdType.MESH
-        )
-        return carry
-
-    lax.fori_loop(1, nblk, greet_blk, 0)
-
-    def greet_grp(d, carry):
-        pl.semaphore_signal(
-            barrier, inc=1, device_id={"grp": lax.rem(y + d, ny) * 2 + xl}, device_id_type=pl.DeviceIdType.MESH
-        )
-        return carry
-
-    lax.fori_loop(1, ny, greet_grp, 0)
-    pl.semaphore_signal(
-        barrier, inc=1, device_id={"grp": y * 2 + 1 - xl}, device_id_type=pl.DeviceIdType.MESH
-    )
+    def greet(where):
+        pl.semaphore_signal(barrier, inc=1, device_id=where, device_id_type=pl.DeviceIdType.MESH)
+
+    def z_dev(d):
+        return {"blk": lax.rem(z + nz + d, nz) * 4 + plane}
+
+    def y_dev(d):
+        return {"grp": lax.rem(y + ny + d, ny) * 2 + xl}
+
+    x_pair = {"grp": y * 2 + 1 - xl}
+    for d in range(1, 4):
+        greet({"blk": z * 4 + lax.rem(plane + d, 4)})
+    for d in (1, -1):
+        greet(z_dev(d))
+        greet({"blk": lax.rem(z + nz + d, nz) * 4 + x_plane})
+    greet(x_pair)
+    for d in range(1, ny):
+        greet(y_dev(d))
+
+    def fetch(n):
+        return pltpu.make_async_copy(given[n], held[n], sem_in.at[n])
+
+    for n in range(10):
+        fetch(n).start()
+    for n in range(10):
+        fetch(n).wait()
 
     my_label = pair_s[g]
     tile_id = lax.div(b, 2)
     same = jnp.where(pair_s[tile_id] == my_label, 1.0, 0.0)
     kept = same * screen_s[g, tile_id].astype(jnp.float32)
-    lad_t = lad[...].T * kept
-    cyc_t = cyc[...].T * same
+    lad_t = lad[...] * kept
+    cyc_t = cyc[...] * same
     for s in range(2):
         psub[s, :, 0:TILE] = lad_t[32 * s : 32 * s + 32]
         psub[s, :, TILE : 2 * TILE] = cyc_t[32 * s : 32 * s + 32]
@@ -81,7 +93,39 @@
     )
     rank = jnp.sum(jnp.where(equal & before, 1.0, 0.0), axis=0, keepdims=True)
     key = irr_v[...].astype(jnp.float32) * occ + rank
-    count_s[0] = jnp.max(rank).astype(jnp.int32) + 1
+    irr_bi = irr_b.astype(jnp.int32)
+    irr_ti = irr_t.astype(jnp.int32)
+    plane_of = lax.broadcasted_iota(jnp.int32, (8, occ), 0) == lax.div(
+        lax.broadcasted_iota(jnp.int32, (8, occ), 1), 4 * ROWS
+    )
+    plane_of = jnp.where(plane_of, 1.0, 0.0)
+    worst = jnp.zeros((8, occ), jnp.float32)
+    for label in range(8):
+        hit = ((irr_bi ^ irr_ti) == label) & (rank < CAP)
+        filled = jnp.dot(
+            plane_of.astype(jnp.bfloat16),
+            jnp.where(hit, 1.0, 0.0).astype(jnp.bfloat16),
+            preferred_element_type=jnp.float32,
+        )
+        worst = jnp.maximum(worst, jnp.sum(filled, axis=1, keepdims=True))
+    count_s[0] = lax.div(jnp.max(rank).astype(jnp.int32) + CAP, CAP)
+    count_s[1] = lax.div(jnp.max(worst).astype(jnp.int32) + JOINT - 1, JOINT)
+    first_rank = (round_s[0] * CAP).astype(jnp.float32)
+
+    def joint_of(label):
+        lane = lax.broadcasted_iota(jnp.int32, (1, 4 * slots), 1)
+        row_of, slot_of = lax.div(lane, CAP), lax.rem(lane, CAP).astype(jnp.float32)
+        irr_f = irr_v[...].astype(jnp.float32)
+        goal = jnp.full((1, 4 * slots), -1.0, jnp.float32)
+        start = jnp.full((1, 1), 0.0, jnp.float32) - (round_s[1] * JOINT).astype(jnp.float32)
+        for row in range(4 * ROWS):
+            want = (irr_s[z * 4 * ROWS + row] ^ label).astype(jnp.float32)
+            fits = (irr_f == want) & (rank >= first_rank) & (rank < first_rank + CAP)
+            size = jnp.sum(jnp.where(fits, 1.0, 0.0), axis=1, keepdims=True)
+            goal = jnp.where((row_of == row) & (slot_of < size), start + slot_of, goal)
+            start = start + size
+        at = lax.broadcasted_iota(jnp.int32, (JOINT, 4 * slots), 0).astype(jnp.float32)
+        return jnp.where(at == jnp.broadcast_to(goal, at.shape), 1.0, 0.0).astype(jnp.bfloat16)
 
     def targets(label, place):
         goal = place.astype(jnp.float32)
@@ -104,7 +148,8 @@
         lhs[plane, rows, 0:TILE] = packed[:CAP]
         lhs[plane, rows, TILE : 2 * TILE] = packed[CAP:]
 
-    pl.semaphore_wait(barrier, nblk - 1 + ny)
+    pack[...] = joint_of(my_label)
+    pl.semaphore_wait(barrier, 8 + ny - 1)
 
     def remote(src, dst, sems, index, where):
         return pltpu.make_async_remote_copy(
@@ -122,37 +167,58 @@
     def from_x():
         return remote(psub.at[1 - h], pan.at[z, 1 - h], sem_b, (0,), {"blk": x_dev})
 
-    def along_z(which, k, d):
+    def to_x_z(way):
+        step = 1 - 2 * way
         return remote(
-            pan.at[z, which], pan.at[z, which], sem_c, (k, d), {"blk": lax.rem(z + d, nz) * 4 + plane}
-        )
+            psub.at[1 - h], pan.at[z, h], sem_c, (1, way, 1),
+            {"blk": lax.rem(z + nz + step, nz) * 4 + x_plane},
+        )
+
+    tiles = (h, 1 - h)
+    reach = ((nz // 2, nz - 1 - nz // 2), (nz - 1 - nz // 2, nz // 2))
+
+    def pass_z(kind, way, t):
+        step = 1 - 2 * way
+        src = lax.rem(z + nz - step * (t - 1), nz)
+        at = pan.at[src, tiles[kind]]
+        return remote(at, at, sem_c, (kind, way, t), z_dev(step))
+
+    def got_z(kind, way, t):
+        step = 1 - 2 * way
+        src = lax.rem(z + nz - step * t, nz)
+        at = pan.at[src, tiles[kind]]
+        return remote(at, at, sem_c, (kind, way, t), z_dev(step))
+
+    def start_z(kind, t):
+        for way in range(2):
+            if t <= reach[kind][way]:
+                if t > 1:
+                    got_z(kind, way, t - 1).wait_recv()
+                pass_z(kind, way, t).start()
 
     def rows_to(src, where, k):
         return remote(lhs.at[src], lhs.at[src], sem_a, (k,), {"blk": where})
 
     to_x().start()
+    for way in range(2):
+        if reach[1][way]:
+            to_x_z(way).start()
+    start_z(0, 1)
     rows_to(plane, x_dev, 0).start()
-
-    def start_own(d, carry):
-        along_z(h, 0, d).start()
-        return carry
-
-    lax.fori_loop(1, nz, start_own, 0)
     rows_to(plane, c_dev, 1).start()
+    for t in range(2, 4):
+        for kind in range(2):
+            start_z(kind, t)
     from_x().wait_recv()
-
-    def start_other(d, carry):
-        along_z(1 - h, 1, d).start()
-        return carry
-
-    lax.fori_loop(1, nz, start_other, 0)
     rows_to(x_plane, x_dev, 0).wait_recv()
     rows_to(x_plane, c_dev, 2).start()
     rows_to(h * 2 + 1 - c, c_dev, 1).wait_recv()
     rows_to((1 - h) * 2 + 1 - c, c_dev, 2).wait_recv()
     hi, lo = split(lhs[...].reshape(4 * slots, 2 * TILE))
-    lhs_hi[...] = hi
-    lhs_lo[...] = lo
+    lhs_hi[...] = jnp.dot(pack[...], hi, preferred_element_type=jnp.float32).astype(jnp.bfloat16)
+    lhs_lo[...] = jnp.dot(pack[...], lo, preferred_element_type=jnp.float32).astype(jnp.bfloat16)
+    out_label = pair_s[order_s[g]]
+    pack[...] = joint_of(out_label)
 
     def multiply(src):
         hi, lo = split(pan[src].reshape(64, 2 * TILE))
@@ -163,45 +229,46 @@
         part[src * 2 + 1] = value[32:]
 
     multiply(z)
-
-    def take_z(d, carry):
-        src = lax.rem(z + nz - d, nz)
-        remote(pan.at[z, h], pan.at[src, h], sem_c, (0, d), {"blk": x_dev}).wait_recv()
-        remote(pan.at[z, h], pan.at[src, 1 - h], sem_c, (1, d), {"blk": x_dev}).wait_recv()
-        multiply(src)
-        return carry
-
-    lax.fori_loop(1, nz, take_z, 0)
+    for t in range(1, nz // 2 + 1):
+        for kind in range(2):
+            if t == 1 and nz // 2 >= 4:
+                for more in range(4, nz // 2 + 1):
+                    start_z(kind, more)
+        for way in range(2):
+            for kind in range(2):
+                if t == reach[kind][way]:
+                    got_z(kind, way, t).wait_recv()
+        multiply(lax.rem(z + nz - t, nz))
+        if 2 * t < nz:
+            multiply(lax.rem(z + t, nz))
 
     def pair_copy(k):
-        return remote(xs.at[k], xb.at[k], sem_x, (k,), {"grp": y * 2 + 1 - xl})
+        return remote(xs.at[k], xb.at[k], sem_x, (k,), x_pair)
 
     def y_copy(k):
-        return remote(ys.at[k], yb.at[k], sem_y, (k,), {"grp": lax.rem(y + k, ny) * 2 + xl})
-
-    def send_x(n, carry):
-        k = lax.rem(n + 1, ny)
-        xs[k] = part[order_s[lax.rem(y + k, ny) * 2 + 1 - xl]]
+        return remote(ys.at[k], yb.at[k], sem_y, (k,), y_dev(k))
+
+    def owner(k):
+        return lax.rem(y + k, ny) * 2
+
+    order = []
+    for far in range(ny // 2, 0, -1):
+        order += [far] if 2 * far == ny else [far, ny - far]
+    for k in order + [0]:
+        xs[k] = part[order_s[owner(k) + 1 - xl]]
         pair_copy(k).start()
-        return carry
-
-    lax.fori_loop(0, ny, send_x, 0)
-
-    def send_y(k, carry):
+    for k in order:
         pair_copy(k).wait_recv()
-        ys[k] = part[order_s[lax.rem(y + k, ny) * 2 + xl]] + xb[k]
+        ys[k] = part[order_s[owner(k) + xl]] + xb[k]
         y_copy(k).start()
-        return carry
-
-    lax.fori_loop(1, ny, send_y, 0)
     pair_copy(0).wait_recv()
     total = part[order_s[g]] + xb[0]
-
-    def take_y(k, total):
+    for k in order:
         y_copy(k).wait_recv()
-        return total + yb[k]
-
-    total = lax.fori_loop(1, ny, take_y, total)
+        total += yb[k]
+    hi, lo = split(total)
+    total = jnp.dot(hi, pack[...], preferred_element_type=jnp.float32)
+    total += jnp.dot(lo, pack[...], preferred_element_type=jnp.float32)
 
     quarter = c * 2 + h
     for r in range(4):
@@ -215,7 +282,6 @@
         plane_copy(d).start()
     full[quarter] = res4[plane]
 
-    out_label = pair_s[order_s[g]]
     key_t = jnp.broadcast_to(key, (slots, occ)).T
     lane = lax.broadcasted_iota(jnp.int32, (occ, slots), 1)
     place = jnp.where(key_t == targets(out_label, lane), 1.0, 0.0)
@@ -242,8 +308,10 @@
             {"blk": to},
         )
 
-    def start_swap(d, carry):
-        swap(d).start()
+    def start_swap(n, carry):
+        odd = lax.rem(n, 2)
+        half = lax.div(n, 2)
+        swap(odd * (half + 1) + (1 - odd) * (nblk - half)).start()
         return carry
 
     lax.fori_loop(1, nblk, start_swap, 0)
@@ -268,20 +336,14 @@
     rows_to(plane, c_dev, 1).wait_send()
     rows_to(x_plane, c_dev, 2).wait_send()
 
-    def end_z(d, carry):
-        along_z(h, 0, d).wait_send()
-        along_z(1 - h, 1, d).wait_send()
-        return carry
-
-    lax.fori_loop(1, nz, end_z, 0)
-    pair_copy(0).wait_send()
-
-    def end_y(k, carry):
+    for kind in range(2):
+        for way in range(2):
+            for t in range(1, reach[kind][way] + 1):
+                (to_x_z(way) if (kind, t) == (1, 1) else pass_z(kind, way, t)).wait_send()
+    for k in order + [0]:
         pair_copy(k).wait_send()
+    for k in order:
         y_copy(k).wait_send()
-        return carry
-
-    lax.fori_loop(1, ny, end_y, 0)
     for d in range(1, 4):
         plane_copy(d).wait_send()
 
@@ -307,29 +369,41 @@
         functools.partial(kernel, nz, ny),
         out_shape=(
             jax.ShapeDtypeStruct((rows, occ, tile), f32),
-            jax.ShapeDtypeStruct((1,), jnp.int32),
+            jax.ShapeDtypeStruct((2,), jnp.int32),
         ),
-        in_specs=[smem] * 5 + [vmem] * 5,
+        in_specs=[pl.BlockSpec(memory_space=pltpu.HBM)] * 10,
         out_specs=(vmem, smem),
         scratch_shapes=[
+            pltpu.SMEM((2,), jnp.int32),
+            pltpu.SMEM(occ_irrep.shape, jnp.int32),
+            pltpu.SMEM(pair_irrep.shape, jnp.int32),
+            pltpu.SMEM(screen.shape, jnp.int32),
+            pltpu.SMEM(block_order.shape, jnp.int32),
+            pltpu.VMEM((1, occ), jnp.int32),
+            pltpu.VMEM((occ, occ), f32),
+            pltpu.VMEM((rows, occ, tile), f32),
+            pltpu.VMEM(ladder_ints.shape[::-1], f32),
+            pltpu.VMEM(cycle_ints.shape[::-1], f32),
             pltpu.VMEM((2, 32, 2 * TILE), f32),
             pltpu.VMEM((nz, 2, 32, 2 * TILE), f32),
             pltpu.VMEM((4, slots, 2 * TILE), f32),
-            pltpu.VMEM((4 * slots, 2 * TILE), jnp.bfloat16),
-            pltpu.VMEM((4 * slots, 2 * TILE), jnp.bfloat16),
-            pltpu.VMEM((2 * nz, 32, 4 * slots), f32),
-            pltpu.VMEM((ny, 32, 4 * slots), f32),
-            pltpu.VMEM((ny, 32, 4 * slots), f32),
-            pltpu.VMEM((ny, 32, 4 * slots), f32),
-            pltpu.VMEM((ny, 32, 4 * slots), f32),
+            pltpu.VMEM((JOINT, 2 * TILE), jnp.bfloat16),
+            pltpu.VMEM((JOINT, 2 * TILE), jnp.bfloat16),
+            pltpu.VMEM((JOINT, 4 * slots), jnp.bfloat16),
+            pltpu.VMEM((2 * nz, 32, JOINT), f32),
+            pltpu.VMEM((ny, 32, JOINT), f32),
+            pltpu.VMEM((ny, 32, JOINT), f32),
+            pltpu.VMEM((ny, 32, JOINT), f32),
+            pltpu.VMEM((ny, 32, JOINT), f32),
             pltpu.VMEM((4, 32, slots), f32),
             pltpu.VMEM((4, 32, slots), f32),
             pltpu.VMEM((rows, occ, tile), f32),
             pltpu.VMEM((rows * occ, tile), f32),
             pltpu.VMEM((rows * occ, tile), f32),
+            dma((10,)),
             dma((2, 3)),
             dma((2, 1)),
-            dma((2, 2, nz)),
+            dma((2, 2, 2, nz // 2 + 1)),
             dma((2, ny)),
             dma((2, ny)),
             dma((2, 4)),
@@ -342,19 +416,20 @@
 
     def part(index):
         return call(
-            jnp.full((1,), index, jnp.int32),
+            index,
             occ_irrep, pair_irrep, screen, block_order, occ_irrep.reshape(1, occ),
-            occ_coupling, amplitudes, ladder_ints, cycle_ints,
-        )
-
-    first, count = part(0)
-    rounds = (count[0] + CAP - 1) // CAP
+            occ_coupling, amplitudes, ladder_ints.T, cycle_ints.T,
+        )
+
+    first, count = part(jnp.zeros((2,), jnp.int32))
+    passes = count[0] * count[1]
 
     def more(state):
-        return state[0] < rounds
+        return state[0] < passes
 
     def again(state):
-        return state[0] + 1, state[1] + part(state[0])[0]
+        index = jnp.stack((state[0] // count[1], state[0] % count[1]))
+        return state[0] + 1, state[1] + part(index)[0]
 
     return lax.while_loop(more, again, (jnp.int32(1), first))[1]
 

time: 69.6 us -> 62.7 us (0.901)
  Pallas kernels: 66.3 us -> 57.1 us
  between operations: 0.74 us -> 3.25 us
    pallas_call x1, Pallas kernels: 66.3 us -> 57.1 us  [part(): call(index, occ_irrep, pair_irrep, screen, block_order, occ_irrep.reshape...]
    unnamed x17, local copies, waits for them, and re-layouts: 2.38 us -> 1.43 us
where the time goes in v2:
time: 62.7 us; the launch traced here: 62.5 us
  Pallas kernels  57.1 us (91%)
  between operations  3.25 us (5%)
  local copies, waits for them, and re-layouts  2.07 us (3%)
    pallas_call x1, Pallas kernels, part(): call(index, occ_irrep, pair_irrep, screen, block_order, occ_irrep.reshape...  57.1 us
    unnamed x17, local copies, waits for them, and re-layouts  1.43 us

profile of v2, /device:TPU:1, one launch (start us, length us, event | category | flops | bytes accessed | tf_op | source)
XLA Modules:
  0.0 62.5 jit_solution(10919435686934789572)
XLA Ops:
  0.0 0.0 copy-start.4
  0.0 0.0 copy-start
  0.0 0.7 %copy-done.4 = s32[16,16]{1,0:T(8,128)S(1)} copy-done((s32[16,16]{1,0:T(8,128)S(1)}, s32[16,16]{1,0:T(8,128)}, u32[]{:S(2)}) %copy-start.4) | copy-done | bytes 1048
  0.7 0.0 copy-start.1
  0.7 0.0 copy-start.2
  0.7 0.0 copy-start.3
  0.7 57.1 %shard_map.82 = (f32[4,128,128]{2,1,0:T(8,128)S(1)}, s32[2]{0:T(128)S(1)}) custom-call(s32[2]{0:T(128)S(1)} %broadcast_1_refs_0_.2.refs_0_, s32[128]{0:T(128)} %refs_1_.1, s32[16]{0:T(128)} %refs_2_.1, s32[16,16]{1,0:T(8,128)S(1)} %copy-done.4, s32[16]{0:T(128)} %refs_4_.1, s32[1,128]{1,0:T(1,128)} %bitcast.27, f32[128,128]{1,0:T(8,128)} %refs_6_.1, ...), custom_call_target="tpu_custom_call" | custom-call | tf_op jit(solution)/shard_map/pallas_call | solution.py:418
  57.8 0.6 %fusion = (s32[1]{0:T(128)}, s32[1]{0:T(128)}) fusion(s32[2]{0:T(128)S(1)} %get-tuple-element.304), kind=kLoop, calls=%fused_computation.1 | loop fusion | bytes 16 | tf_op jit(solution)/shard_map/slice | solution.py:425
  60.4 0.0 copy-start.5
  60.4 0.0 copy-start.6
  60.4 0.0 copy-start.7
  61.7 0.0 copy-done
  61.7 0.0 copy-done.1
  61.7 0.0 copy-done.2
  61.7 0.0 copy-done.3
  61.7 0.0 copy-done.5
  61.7 0.0 copy-done.6
  61.7 0.0 copy-done.7
  61.8 0.7 %copy.16 = f32[4,128,128]{2,1,0:T(8,128)} copy(f32[4,128,128]{2,1,0:T(8,128)S(1)} %get-tuple-element.173) | data formatting | bytes 524288
  (2 shorter events, 0.0 us)
Async XLA Ops:
  0.0 0.7 %copy-start.4 = (s32[16,16]{1,0:T(8,128)S(1)}, s32[16,16]{1,0:T(8,128)}, u32[]{:S(2)}) copy-start(s32[16,16]{1,0:T(8,128)} %refs_3_.1) | copy-start | bytes 3076
  0.0 61.7 %copy-start = (f32[4,128,128]{2,1,0:T(8,128)S(1)}, f32[4,128,128]{2,1,0:T(8,128)}, u32[]{:S(2)}) copy-start(f32[4,128,128]{2,1,0:T(8,128)} %refs_7_.1) | copy-start | bytes 786436
  0.7 61.0 %copy-start.1 = (f32[128,128]{1,0:T(8,128)S(1)}, f32[128,128]{1,0:T(8,128)}, u32[]{:S(2)}) copy-start(f32[128,128]{1,0:T(8,128)} %refs_6_.1) | copy-start | bytes 196612
  0.7 61.0 %copy-start.2 = (f32[128,64]{0,1:T(8,128)S(1)}, f32[128,64]{0,1:T(8,128)}, u32[]{:S(2)}) copy-start(f32[128,64]{0,1:T(8,128)} %param.11) | copy-start | bytes 98308
  0.7 61.0 %copy-start.3 = (f32[128,64]{0,1:T(8,128)S(1)}, f32[128,64]{0,1:T(8,128)}, u32[]{:S(2)}) copy-start(f32[128,64]{0,1:T(8,128)} %param.12) | copy-start | bytes 98308
  60.4 1.4 %copy-start.5 = (s32[128]{0:T(128)S(1)}, s32[128]{0:T(128)}, u32[]{:S(2)}) copy-start(s32[128]{0:T(128)} %refs_1_.1) | copy-start | bytes 1540
  60.4 1.4 %copy-start.6 = (s32[16]{0:T(128)S(1)}, s32[16]{0:T(128)}, u32[]{:S(2)}) copy-start(s32[16]{0:T(128)} %refs_2_.1) | copy-start | bytes 196
  60.4 1.4 %copy-start.7 = (s32[16]{0:T(128)S(1)}, s32[16]{0:T(128)}, u32[]{:S(2)}) copy-start(s32[16]{0:T(128)} %refs_4_.1) | copy-start | bytes 196

commit v3 on v2

v3 whole, which is shorter than its diff:
```python
import functools

import jax
import jax.numpy as jnp
import numpy as np
from jax import lax
from jax.experimental import pallas as pl
from jax.experimental.pallas import tpu as pltpu
from jax.sharding import PartitionSpec as P

CAP = 32
JOINT = 384
ROWS = 4
TILE = 128
NT = (((1,), (1,)), ((), ()))
NN = (((1,), (0,)), ((), ()))


def split(x):
    hi = x.astype(jnp.bfloat16)
    return hi, (x - hi.astype(jnp.float32)).astype(jnp.bfloat16)


def product(a, b, dims):
    a_hi, a_lo = split(a)
    b_hi, b_lo = split(b)
    value = lax.dot_general(a_hi, b_hi, dims, preferred_element_type=jnp.float32)
    value += lax.dot_general(a_hi, b_lo, dims, preferred_element_type=jnp.float32)
    return value + lax.dot_general(a_lo, b_hi, dims, preferred_element_type=jnp.float32)


def kernel(
    nz, ny,
    *refs,
):
    given, (out, count_s), held = refs[:10], refs[10:12], refs[12:22]
    round_s, irr_s, pair_s, screen_s, order_s, irr_v, coup, amps, lad, cyc = held
    (
        psub, pan, lhs, lhs_hi, lhs_lo, pack, place, part, xs, xb, ys, yb, res4, full, own, send, back,
        sem_in, sem_a, sem_b, sem_c, sem_x, sem_y, sem_f, sem_h,
    ) = refs[22:]
    nblk = 4 * nz
    occ = amps.shape[1]
    slots = ROWS * CAP
    g = lax.axis_index("grp")
    b = lax.axis_index("blk")
    z = lax.div(b, 4)
    plane = lax.rem(b, 4)
    h = lax.div(plane, 2)
    c = lax.rem(plane, 2)
    y = lax.div(g, 2)
    xl = lax.rem(g, 2)
    x_dev = z * 4 + (1 - h) * 2 + c
    c_dev = z * 4 + h * 2 + (1 - c)
    x_plane = (1 - h) * 2 + c

    barrier = pltpu.get_barrier_semaphore()

    def greet(where):
        pl.semaphore_signal(barrier, inc=1, device_id=where, device_id_type=pl.DeviceIdType.MESH)

    def z_dev(d):
        return {"blk": lax.rem(z + nz + d, nz) * 4 + plane}

    def y_dev(d):
        return {"grp": lax.rem(y + ny + d, ny) * 2 + xl}

    x_pair = {"grp": y * 2 + 1 - xl}
    for d in range(1, 4):
        greet({"blk": z * 4 + lax.rem(plane + d, 4)})
    for d in (1, -1):
        greet(z_dev(d))
        greet({"blk": lax.rem(z + nz + d, nz) * 4 + x_plane})
    greet(x_pair)
    for d in range(1, ny):
        greet(y_dev(d))

    def fetch(n):
        return pltpu.make_async_copy(given[n], held[n], sem_in.at[n])

    for n in (8, 9, 2, 3, 1, 4, 0, 5, 6, 7):
        fetch(n).start()
    for n in (2, 3, 8, 9):
        fetch(n).wait()

    my_label = pair_s[g]
    tile_id = lax.div(b, 2)
    same = jnp.where(pair_s[tile_id] == my_label, 1.0, 0.0)
    kept = same * screen_s[g, tile_id].astype(jnp.float32)
    lad_t = lad[...] * kept
    cyc_t = cyc[...] * same
    for s in range(2):
        psub[s, :, 0:TILE] = lad_t[32 * s : 32 * s + 32]
        psub[s, :, TILE : 2 * TILE] = cyc_t[32 * s : 32 * s + 32]
    pan[z, h] = psub[h]

    pl.semaphore_wait(barrier, 8 + ny - 1)

    def remote(src, dst, sems, index, where):
        return pltpu.make_async_remote_copy(
            src_ref=src,
            dst_ref=dst,
            send_sem=sems.at[(0, *index)],
            recv_sem=sems.at[(1, *index)],
            device_id=where,
            device_id_type=pl.DeviceIdType.MESH,
        )

    def to_x():
        return remote(psub.at[1 - h], pan.at[z, h], sem_b, (0,), {"blk": x_dev})

    def from_x():
        return remote(psub.at[1 - h], pan.at[z, 1 - h], sem_b, (0,), {"blk": x_dev})

    def to_x_z(way):
        step = 1 - 2 * way
        return remote(
            psub.at[1 - h], pan.at[z, h], sem_c, (1, way, 1),
            {"blk": lax.rem(z + nz + step, nz) * 4 + x_plane},
        )

    tiles = (h, 1 - h)
    reach = ((nz // 2, nz - 1 - nz // 2), (nz - 1 - nz // 2, nz // 2))

    def pass_z(kind, way, t):
        step = 1 - 2 * way
        src = lax.rem(z + nz - step * (t - 1), nz)
        at = pan.at[src, tiles[kind]]
        return remote(at, at, sem_c, (kind, way, t), z_dev(step))

    def got_z(kind, way, t):
        step = 1 - 2 * way
        src = lax.rem(z + nz - step * t, nz)
        at = pan.at[src, tiles[kind]]
        return remote(at, at, sem_c, (kind, way, t), z_dev(step))

    def start_z(kind, t):
        for way in range(2):
            if t <= reach[kind][way]:
                if t > 1:
                    got_z(kind, way, t - 1).wait_recv()
                pass_z(kind, way, t).start()

    def rows_to(src, where, k):
        return remote(lhs.at[src], lhs.at[src], sem_a, (k,), {"blk": where})

    to_x().start()
    for way in range(2):
        if reach[1][way]:
            to_x_z(way).start()
    start_z(0, 1)
    for n in (0, 1, 4, 5, 6, 7):
        fetch(n).wait()

    irr_b = jnp.broadcast_to(irr_v[...].astype(jnp.float32), (occ, occ))
    irr_t = irr_b.T
    equal = irr_b == irr_t
    before = lax.broadcasted_iota(jnp.int32, (occ, occ), 0) < lax.broadcasted_iota(
        jnp.int32, (occ, occ), 1
    )
    rank = jnp.sum(jnp.where(equal & before, 1.0, 0.0), axis=0, keepdims=True)
    key = irr_v[...].astype(jnp.float32) * occ + rank
    first_rank = (round_s[0] * CAP).astype(jnp.float32)

    def joint_of(label):
        lane = lax.broadcasted_iota(jnp.int32, (1, 4 * slots), 1)
        row_of, slot_of = lax.div(lane, CAP), lax.rem(lane, CAP).astype(jnp.float32)
        irr_f = irr_v[...].astype(jnp.float32)
        goal = jnp.full((1, 4 * slots), -1.0, jnp.float32)
        start = jnp.full((1, 1), 0.0, jnp.float32) - (round_s[1] * JOINT).astype(jnp.float32)
        for row in range(4 * ROWS):
            want = (irr_s[z * 4 * ROWS + row] ^ label).astype(jnp.float32)
            fits = (irr_f == want) & (rank >= first_rank) & (rank < first_rank + CAP)
            size = jnp.sum(jnp.where(fits, 1.0, 0.0), axis=1, keepdims=True)
            goal = jnp.where((row_of == row) & (slot_of < size), start + slot_of, goal)
            start = start + size
        at = lax.broadcasted_iota(jnp.int32, (JOINT, 4 * slots), 0).astype(jnp.float32)
        return jnp.where(at == jnp.broadcast_to(goal, at.shape), 1.0, 0.0).astype(jnp.bfloat16)

    def targets(label, place):
        goal = place.astype(jnp.float32)
        for i in reversed(range(ROWS)):
            base = (irr_s[b * ROWS + i] ^ label) * occ + round_s[0] * CAP - CAP * i
            at = place.astype(jnp.float32) + base.astype(jnp.float32)
            goal = at if i == ROWS - 1 else jnp.where(place < CAP * (i + 1), at, goal)
        return goal

    key_b = jnp.broadcast_to(key, (slots, occ))
    sel = jnp.where(
        key_b == targets(my_label, lax.broadcasted_iota(jnp.int32, (slots, occ), 0)), 1.0, 0.0
    )
    coupling = jnp.where(equal, coup[...], 0.0)
    sel_c = product(sel, coupling, NT)
    for i in range(ROWS):
        rows = slice(CAP * i, CAP * i + CAP)
        pick = jnp.concatenate((sel[rows], sel_c[rows]), axis=0)
        packed = product(pick, amps[i], NN)
        lhs[plane, rows, 0:TILE] = packed[:CAP]
        lhs[plane, rows, TILE : 2 * TILE] = packed[CAP:]

    rows_to(plane, x_dev, 0).start()
    rows_to(plane, c_dev, 1).start()
    for kind in range(2):
        start_z(kind, 2)
    pack[...] = joint_of(my_label)
    for kind in range(2):
        start_z(kind, 3)
    from_x().wait_recv()
    rows_to(x_plane, x_dev, 0).wait_recv()
    rows_to(x_plane, c_dev, 2).start()
    rows_to(h * 2 + 1 - c, c_dev, 1).wait_recv()
    rows_to((1 - h) * 2 + 1 - c, c_dev, 2).wait_recv()
    hi, lo = split(lhs[...].reshape(4 * slots, 2 * TILE))
    lhs_hi[...] = jnp.dot(pack[...], hi, preferred_element_type=jnp.float32).astype(jnp.bfloat16)
    lhs_lo[...] = jnp.dot(pack[...], lo, preferred_element_type=jnp.float32).astype(jnp.bfloat16)

    def multiply(src):
        hi, lo = split(pan[src].reshape(64, 2 * TILE))
        value = lax.dot_general(hi, lhs_hi[...], NT, preferred_element_type=jnp.float32)
        value += lax.dot_general(hi, lhs_lo[...], NT, preferred_element_type=jnp.float32)
        value += lax.dot_general(lo, lhs_hi[...], NT, preferred_element_type=jnp.float32)
        part[src * 2] = value[:32]
        part[src * 2 + 1] = value[32:]

    multiply(z)
    for t in range(1, nz // 2 + 1):
        for kind in range(2):
            if t == 1 and nz // 2 >= 4:
                for more in range(4, nz // 2 + 1):
                    start_z(kind, more)
        for way in range(2):
            for kind in range(2):
                if t == reach[kind][way]:
                    got_z(kind, way, t).wait_recv()
        multiply(lax.rem(z + nz - t, nz))
        if 2 * t < nz:
            multiply(lax.rem(z + t, nz))

    def pair_copy(k):
        return remote(xs.at[k], xb.at[k], sem_x, (k,), x_pair)

    def y_copy(k):
        return remote(ys.at[k], yb.at[k], sem_y, (k,), y_dev(k))

    def owner(k):
        return lax.rem(y + k, ny) * 2

    order = []
    for far in range(ny // 2, 0, -1):
        order += [far] if 2 * far == ny else [far, ny - far]
    for k in order + [0]:
        xs[k] = part[order_s[owner(k) + 1 - xl]]
        pair_copy(k).start()
    for k in order:
        pair_copy(k).wait_recv()
        ys[k] = part[order_s[owner(k) + xl]] + xb[k]
        y_copy(k).start()
    out_label = pair_s[order_s[g]]
    pack[...] = joint_of(out_label)
    key_t = jnp.broadcast_to(key, (slots, occ)).T
    lane = lax.broadcasted_iota(jnp.int32, (occ, slots), 1)
    where = key_t == targets(out_label, lane)
    for i in range(ROWS):
        mine = where & (lane >= CAP * i) & (lane < CAP * (i + 1))
        place[occ * i : occ * (i + 1)] = jnp.where(mine, 1.0, 0.0).astype(jnp.bfloat16)
    pair_copy(0).wait_recv()
    total = part[order_s[g]] + xb[0]
    for k in order:
        y_copy(k).wait_recv()
        total += yb[k]
    hi, lo = split(total)
    total = jnp.dot(hi, pack[...], preferred_element_type=jnp.float32)
    total += jnp.dot(lo, pack[...], preferred_element_type=jnp.float32)

    quarter = c * 2 + h
    for r in range(4):
        res4[r] = total[:, slots * r : slots * (r + 1)]

    def plane_copy(d):
        to = lax.rem(plane + d, 4)
        return remote(res4.at[to], full.at[quarter], sem_f, (d,), {"blk": z * 4 + to})

    for d in range(1, 4):
        plane_copy(d).start()
    full[quarter] = res4[plane]

    for d in range(1, 4):
        other = lax.rem(plane + 4 - d, 4)
        other_quarter = lax.rem(other, 2) * 2 + lax.div(other, 2)
        remote(res4.at[0], full.at[other_quarter], sem_f, (d,), {"blk": c_dev}).wait_recv()
    hi, lo = split(full[...].reshape(TILE, slots).T)
    value = jnp.dot(place[...], hi, preferred_element_type=jnp.float32)
    value += jnp.dot(place[...], lo, preferred_element_type=jnp.float32)
    for i in range(ROWS):
        own[i] = value[occ * i : occ * (i + 1)]
        send[pl.ds(i, occ, stride=ROWS), :] = value[occ * i : occ * (i + 1)]

    def swap(d):
        to = lax.rem(b + d, nblk)
        return remote(
            send.at[pl.ds(pl.multiple_of(to * 16, 16), 16)],
            back.at[pl.ds(pl.multiple_of(b * 16, 16), 16)],
            sem_h,
            (d,),
            {"blk": to},
        )

    def start_swap(n, carry):
        odd = lax.rem(n, 2)
        half = lax.div(n, 2)
        swap(odd * (half + 1) + (1 - odd) * (nblk - half)).start()
        return carry

    lax.fori_loop(1, nblk, start_swap, 0)
    here = pl.ds(pl.multiple_of(b * 16, 16), 16)
    back[here] = send[here]

    irr_bi = irr_b.astype(jnp.int32)
    irr_ti = irr_t.astype(jnp.int32)
    plane_of = lax.broadcasted_iota(jnp.int32, (8, occ), 0) == lax.div(
        lax.broadcasted_iota(jnp.int32, (8, occ), 1), 4 * ROWS
    )
    plane_of = jnp.where(plane_of, 1.0, 0.0)
    worst = jnp.zeros((8, occ), jnp.float32)
    for label in range(8):
        hit = ((irr_bi ^ irr_ti) == label) & (rank < CAP)
        filled = jnp.dot(
            plane_of.astype(jnp.bfloat16),
            jnp.where(hit, 1.0, 0.0).astype(jnp.bfloat16),
            preferred_element_type=jnp.float32,
        )
        worst = jnp.maximum(worst, jnp.sum(filled, axis=1, keepdims=True))
    chunks = lax.div(jnp.max(worst).astype(jnp.int32) + JOINT - 1, JOINT)
    count_s[0] = lax.div(jnp.max(rank).astype(jnp.int32) + CAP, CAP) * chunks
    count_s[1] = chunks

    def take_swap(d, carry):
        src = lax.rem(b + nblk - d, nblk)
        remote(
            send.at[here], back.at[pl.ds(pl.multiple_of(src * 16, 16), 16)], sem_h, (d,), {"blk": c_dev}
        ).wait_recv()
        return carry

    lax.fori_loop(1, nblk, take_swap, 0)
    for j in range(ROWS):
        for i in range(ROWS):
            at = pl.ds(i, nblk, stride=ROWS)
            out[j, at, :] = own[j, at, :] - back[pl.ds(ROWS * j + i, nblk, stride=16), :]

    to_x().wait_send()
    rows_to(plane, x_dev, 0).wait_send()
    rows_to(plane, c_dev, 1).wait_send()
    rows_to(x_plane, c_dev, 2).wait_send()

    for kind in range(2):
        for way in range(2):
            for t in range(1, reach[kind][way] + 1):
                (to_x_z(way) if (kind, t) == (1, 1) else pass_z(kind, way, t)).wait_send()
    for k in order + [0]:
        pair_copy(k).wait_send()
    for k in order:
        y_copy(k).wait_send()
    for d in range(1, 4):
        plane_copy(d).wait_send()

    def end_swap(d, carry):
        swap(d).wait_send()
        return carry

    lax.fori_loop(1, nblk, end_swap, 0)


def shards(
    amplitudes, ladder_ints, cycle_ints, occ_coupling, occ_irrep, pair_irrep, screen, block_order
):
    rows, occ, tile = amplitudes.shape
    nz = lax.axis_size("blk") // 4
    ny = lax.axis_size("grp") // 2
    slots = ROWS * CAP
    f32 = jnp.float32
    smem = pl.BlockSpec(memory_space=pltpu.SMEM)
    vmem = pl.BlockSpec(memory_space=pltpu.VMEM)
    dma = pltpu.SemaphoreType.DMA
    call = pl.pallas_call(
        functools.partial(kernel, nz, ny),
        out_shape=(
            jax.ShapeDtypeStruct((rows, occ, tile), f32),
            jax.ShapeDtypeStruct((2,), jnp.int32),
        ),
        in_specs=[pl.BlockSpec(memory_space=pltpu.HBM)] * 10,
        out_specs=(vmem, smem),
        scratch_shapes=[
            pltpu.SMEM((3,), jnp.int32),
            pltpu.SMEM(occ_irrep.shape, jnp.int32),
            pltpu.SMEM(pair_irrep.shape, jnp.int32),
            pltpu.SMEM(screen.shape, jnp.int32),
            pltpu.SMEM(block_order.shape, jnp.int32),
            pltpu.VMEM((1, occ), jnp.int32),
            pltpu.VMEM((occ, occ), f32),
            pltpu.VMEM((rows, occ, tile), f32),
            pltpu.VMEM(ladder_ints.shape[::-1], f32),
            pltpu.VMEM(cycle_ints.shape[::-1], f32),
            pltpu.VMEM((2, 32, 2 * TILE), f32),
            pltpu.VMEM((nz, 2, 32, 2 * TILE), f32),
            pltpu.VMEM((4, slots, 2 * TILE), f32),
            pltpu.VMEM((JOINT, 2 * TILE), jnp.bfloat16),
            pltpu.VMEM((JOINT, 2 * TILE), jnp.bfloat16),
            pltpu.VMEM((JOINT, 4 * slots), jnp.bfloat16),
            pltpu.VMEM((rows * occ, slots), jnp.bfloat16),
            pltpu.VMEM((2 * nz, 32, JOINT), f32),
            pltpu.VMEM((ny, 32, JOINT), f32),
            pltpu.VMEM((ny, 32, JOINT), f32),
            pltpu.VMEM((ny, 32, JOINT), f32),
            pltpu.VMEM((ny, 32, JOINT), f32),
            pltpu.VMEM((4, 32, slots), f32),
            pltpu.VMEM((4, 32, slots), f32),
            pltpu.VMEM((rows, occ, tile), f32),
            pltpu.VMEM((rows * occ, tile), f32),
            pltpu.VMEM((rows * occ, tile), f32),
            dma((10,)),
            dma((2, 3)),
            dma((2, 1)),
            dma((2, 2, 2, nz // 2 + 1)),
            dma((2, ny)),
            dma((2, ny)),
            dma((2, 4)),
            dma((2, 4 * nz)),
        ],
        compiler_params=pltpu.CompilerParams(
            collective_id=0, has_side_effects=True, vmem_limit_bytes=24 << 20
        ),
    )

    def part(index):
        return call(
            index,
            occ_irrep, pair_irrep, screen, block_order, occ_irrep.reshape(1, occ),
            occ_coupling, amplitudes, ladder_ints.T, cycle_ints.T,
        )

    first, count = part(np.array((0, 0, 1), np.int32))

    def more(state):
        return state[0] < count[0]

    def again(state):
        index = jnp.stack((lax.div(state[0], count[1]), lax.rem(state[0], count[1]), jnp.int32(1)))
        return state[0] + 1, state[1] + part(index)[0]

    def rest(value):
        return lax.while_loop(more, again, (jnp.int32(1), value))[1]

    return lax.cond(count[0] > 1, rest, lambda value: value, first)


def solution(mesh):
    placed = (P("blk", None, "grp"), P("grp", "blk"), P("grp", "blk"), P(), P(), P(), P(), P())
    return jax.shard_map(
        shards, mesh=mesh, in_specs=placed, out_specs=P("blk", None, "grp"), check_vma=False
    )
```

time: 62.7 us -> 59 us (0.941)
  between operations: 3.25 us -> 0.65 us
    slice x1 -> x0, local copies, waits for them, and re-layouts: 0.64 us -> none  [shards(): passes = count[0] * count[1]]
    unnamed x17 -> x19, local copies, waits for them, and re-layouts: 1.43 us -> 1.47 us
where the time goes in v3:
time: 59 us; the launch traced here: 58.9 us
  Pallas kernels  56.7 us (96%)
  local copies, waits for them, and re-layouts  1.47 us (2%)
  between operations  0.65 us (1%)
    pallas_call x1, Pallas kernels, part(): call(index, occ_irrep, pair_irrep, screen, block_order, occ_irrep.reshape...  56.7 us
    unnamed x19, local copies, waits for them, and re-layouts  1.47 us

profile of v3, /device:TPU:1, one launch (start us, length us, event | category | flops | bytes accessed | tf_op | source)
XLA Modules:
  0.0 58.9 jit_solution(4901183004197366694)
XLA Ops:
  0.0 0.0 copy-start.6
  0.0 0.0 copy-start.7
  0.0 0.0 copy-start.8
  0.0 0.0 copy-start
  0.0 0.0 copy-start.1
  0.0 0.6 %copy-done.6 = s32[128]{0:T(128)S(1)} copy-done((s32[128]{0:T(128)S(1)}, s32[128]{0:T(128)}, u32[]{:S(2)}) %copy-start.6) | copy-done | bytes 536
  0.7 0.0 copy-done.7
  0.7 0.0 copy-done.8
  0.7 0.0 copy-done
  0.7 0.0 copy-start.2
  0.7 0.0 copy-start.3
  0.7 0.0 copy-start.4
  0.7 56.7 %shard_map.93 = (f32[4,128,128]{2,1,0:T(8,128)S(1)}, s32[2]{0:T(128)}) custom-call(s32[3]{0:T(128)S(1)} %copy-done, s32[128]{0:T(128)S(1)} %copy-done.6, s32[16]{0:T(128)S(1)} %copy-done.7, s32[16,16]{1,0:T(8,128)} %refs_3_.1, s32[16]{0:T(128)S(1)} %copy-done.8, s32[1,128]{1,0:T(1,128)S(1)} %bitcast.31, f32[128,128]{1,0:T(8,128)} %refs_6_.1, ...), custom_call_target="tpu_custom_call" | custom-call | tf_op jit(solution)/shard_map/pallas_call | solution.py:435
  57.4 0.0 copy-start.5
  58.0 0.0 copy-done.1
  58.0 0.0 copy-done.2
  58.1 0.0 copy-done.3
  58.1 0.0 copy-done.4
  58.1 0.1 copy-done.5
  58.2 0.7 %copy.21 = f32[4,128,128]{2,1,0:T(8,128)} copy(f32[4,128,128]{2,1,0:T(8,128)S(1)} %get-tuple-element.102) | data formatting | bytes 524288
  (1 shorter events, 0.0 us)
Async XLA Ops:
  0.0 0.7 %copy-start.6 = (s32[128]{0:T(128)S(1)}, s32[128]{0:T(128)}, u32[]{:S(2)}) copy-start(s32[128]{0:T(128)} %refs_1_.1) | copy-start | bytes 1540
  0.0 0.7 %copy-start.7 = (s32[16]{0:T(128)S(1)}, s32[16]{0:T(128)}, u32[]{:S(2)}) copy-start(s32[16]{0:T(128)} %refs_2_.1) | copy-start | bytes 196
  0.0 0.7 %copy-start.8 = (s32[16]{0:T(128)S(1)}, s32[16]{0:T(128)}, u32[]{:S(2)}) copy-start(s32[16]{0:T(128)} %refs_4_.1) | copy-start | bytes 196
  0.0 0.7 %copy-start = (s32[3]{0:T(128)S(1)}, s32[3]{0:T(128)}, u32[]{:S(2)}) copy-start(s32[3]{0:T(128)} %constant.11.clone.refs_0_) | copy-start | bytes 40
  0.0 58.0 %copy-start.1 = (f32[4,128,128]{2,1,0:T(8,128)S(1)}, f32[4,128,128]{2,1,0:T(8,128)}, u32[]{:S(2)}) copy-start(f32[4,128,128]{2,1,0:T(8,128)} %refs_7_.1) | copy-start | bytes 786436
  0.7 57.3 %copy-start.2 = (f32[128,128]{1,0:T(8,128)S(1)}, f32[128,128]{1,0:T(8,128)}, u32[]{:S(2)}) copy-start(f32[128,128]{1,0:T(8,128)} %refs_6_.1) | copy-start | bytes 196612
  0.7 57.4 %copy-start.3 = (f32[128,64]{0,1:T(8,128)S(1)}, f32[128,64]{0,1:T(8,128)}, u32[]{:S(2)}) copy-start(f32[128,64]{0,1:T(8,128)} %param.14) | copy-start | bytes 98308
  0.7 57.4 %copy-start.4 = (f32[128,64]{0,1:T(8,128)S(1)}, f32[128,64]{0,1:T(8,128)}, u32[]{:S(2)}) copy-start(f32[128,64]{0,1:T(8,128)} %param.15) | copy-start | bytes 98308
  57.4 0.7 %copy-start.5 = (s32[16,16]{1,0:T(8,128)S(1)}, s32[16,16]{1,0:T(8,128)}, u32[]{:S(2)}) copy-start(s32[16,16]{1,0:T(8,128)} %refs_3_.1) | copy-start | bytes 3076

commit v4 on v3

--- a/solution.py
+++ b/solution.py
@@ -208,6 +208,9 @@
     from_x().wait_recv()
     rows_to(x_plane, x_dev, 0).wait_recv()
     rows_to(x_plane, c_dev, 2).start()
+    for kind in range(2):
+        for t in range(4, nz // 2 + 1):
+            start_z(kind, t)
     rows_to(h * 2 + 1 - c, c_dev, 1).wait_recv()
     rows_to((1 - h) * 2 + 1 - c, c_dev, 2).wait_recv()
     hi, lo = split(lhs[...].reshape(4 * slots, 2 * TILE))
@@ -224,10 +227,6 @@
 
     multiply(z)
     for t in range(1, nz // 2 + 1):
-        for kind in range(2):
-            if t == 1 and nz // 2 >= 4:
-                for more in range(4, nz // 2 + 1):
-                    start_z(kind, more)
         for way in range(2):
             for kind in range(2):
                 if t == reach[kind][way]:
@@ -301,11 +300,16 @@
             send.at[pl.ds(pl.multiple_of(to * 16, 16), 16)],
             back.at[pl.ds(pl.multiple_of(b * 16, 16), 16)],
             sem_h,
-            (d,),
+            (0,),
             {"blk": to},
         )
 
-    def start_swap(n, carry):
+    def all_swaps():
+        most = pl.ds(0, 16 * (nblk - 1))
+        return remote(send.at[most], back.at[most], sem_h, (0,), {"blk": c_dev})
+
+    def start_swap(m, carry):
+        n = nblk - m
         odd = lax.rem(n, 2)
         half = lax.div(n, 2)
         swap(odd * (half + 1) + (1 - odd) * (nblk - half)).start()
@@ -334,19 +338,6 @@
     count_s[0] = lax.div(jnp.max(rank).astype(jnp.int32) + CAP, CAP) * chunks
     count_s[1] = chunks
 
-    def take_swap(d, carry):
-        src = lax.rem(b + nblk - d, nblk)
-        remote(
-            send.at[here], back.at[pl.ds(pl.multiple_of(src * 16, 16), 16)], sem_h, (d,), {"blk": c_dev}
-        ).wait_recv()
-        return carry
-
-    lax.fori_loop(1, nblk, take_swap, 0)
-    for j in range(ROWS):
-        for i in range(ROWS):
-            at = pl.ds(i, nblk, stride=ROWS)
-            out[j, at, :] = own[j, at, :] - back[pl.ds(ROWS * j + i, nblk, stride=16), :]
-
     to_x().wait_send()
     rows_to(plane, x_dev, 0).wait_send()
     rows_to(plane, c_dev, 1).wait_send()
@@ -362,12 +353,13 @@
         y_copy(k).wait_send()
     for d in range(1, 4):
         plane_copy(d).wait_send()
-
-    def end_swap(d, carry):
-        swap(d).wait_send()
-        return carry
-
-    lax.fori_loop(1, nblk, end_swap, 0)
+    all_swaps().wait_recv()
+    for j in range(ROWS):
+        for i in range(ROWS):
+            at = pl.ds(i, nblk, stride=ROWS)
+            out[j, at, :] = own[j, at, :] - back[pl.ds(ROWS * j + i, nblk, stride=16), :]
+
+    all_swaps().wait_send()
 
 
 def shards(
@@ -424,7 +416,7 @@
             dma((2, ny)),
             dma((2, ny)),
             dma((2, 4)),
-            dma((2, 4 * nz)),
+            dma((2, 1)),
         ],
         compiler_params=pltpu.CompilerParams(
             collective_id=0, has_side_effects=True, vmem_limit_bytes=24 << 20

time: 59 us -> 58.1 us (0.985)
  Pallas kernels: 56.7 us -> 55.8 us
    pallas_call x1, Pallas kernels: 56.7 us -> 55.8 us  [part(): call(index, occ_irrep, pair_irrep, screen, block_order, occ_irrep.reshape...]
where the time goes in v4:
time: 58.1 us; the launch traced here: 57.9 us
  Pallas kernels  55.8 us (96%)
  local copies, waits for them, and re-layouts  1.47 us (3%)
  between operations  0.65 us (1%)
    pallas_call x1, Pallas kernels, part(): call(index, occ_irrep, pair_irrep, screen, block_order, occ_irrep.reshape...  55.8 us
    unnamed x19, local copies, waits for them, and re-layouts  1.47 us

profile of v4, /device:TPU:1, one launch (start us, length us, event | category | flops | bytes accessed | tf_op | source)
XLA Modules:
  0.0 57.9 jit_solution(6233088814325881357)
XLA Ops:
  0.0 0.0 copy-start.6
  0.0 0.0 copy-start.7
  0.0 0.0 copy-start.8
  0.0 0.0 copy-start
  0.0 0.0 copy-start.1
  0.0 0.6 %copy-done.6 = s32[128]{0:T(128)S(1)} copy-done((s32[128]{0:T(128)S(1)}, s32[128]{0:T(128)}, u32[]{:S(2)}) %copy-start.6) | copy-done | bytes 536
  0.7 0.0 copy-done.7
  0.7 0.0 copy-done.8
  0.7 0.0 copy-done
  0.7 0.0 copy-start.2
  0.7 0.0 copy-start.3
  0.7 0.0 copy-start.4
  0.7 55.8 %shard_map.93 = (f32[4,128,128]{2,1,0:T(8,128)S(1)}, s32[2]{0:T(128)}) custom-call(s32[3]{0:T(128)S(1)} %copy-done, s32[128]{0:T(128)S(1)} %copy-done.6, s32[16]{0:T(128)S(1)} %copy-done.7, s32[16,16]{1,0:T(8,128)} %refs_3_.1, s32[16]{0:T(128)S(1)} %copy-done.8, s32[1,128]{1,0:T(1,128)S(1)} %bitcast.31, f32[128,128]{1,0:T(8,128)} %refs_6_.1, ...), custom_call_target="tpu_custom_call" | custom-call | tf_op jit(solution)/shard_map/pallas_call | solution.py:427
  56.5 0.0 copy-start.5
  57.1 0.0 copy-done.1
  57.1 0.0 copy-done.2
  57.1 0.0 copy-done.3
  57.1 0.0 copy-done.4
  57.2 0.1 copy-done.5
  57.2 0.7 %copy.21 = f32[4,128,128]{2,1,0:T(8,128)} copy(f32[4,128,128]{2,1,0:T(8,128)S(1)} %get-tuple-element.102) | data formatting | bytes 524288
  (1 shorter events, 0.0 us)
Async XLA Ops:
  0.0 0.7 %copy-start.6 = (s32[128]{0:T(128)S(1)}, s32[128]{0:T(128)}, u32[]{:S(2)}) copy-start(s32[128]{0:T(128)} %refs_1_.1) | copy-start | bytes 1540
  0.0 0.7 %copy-start.7 = (s32[16]{0:T(128)S(1)}, s32[16]{0:T(128)}, u32[]{:S(2)}) copy-start(s32[16]{0:T(128)} %refs_2_.1) | copy-start | bytes 196
  0.0 0.7 %copy-start.8 = (s32[16]{0:T(128)S(1)}, s32[16]{0:T(128)}, u32[]{:S(2)}) copy-start(s32[16]{0:T(128)} %refs_4_.1) | copy-start | bytes 196
  0.0 0.7 %copy-start = (s32[3]{0:T(128)S(1)}, s32[3]{0:T(128)}, u32[]{:S(2)}) copy-start(s32[3]{0:T(128)} %constant.11.clone.refs_0_) | copy-start | bytes 40
  0.0 57.1 %copy-start.1 = (f32[4,128,128]{2,1,0:T(8,128)S(1)}, f32[4,128,128]{2,1,0:T(8,128)}, u32[]{:S(2)}) copy-start(f32[4,128,128]{2,1,0:T(8,128)} %refs_7_.1) | copy-start | bytes 786436
  0.7 56.4 %copy-start.2 = (f32[128,128]{1,0:T(8,128)S(1)}, f32[128,128]{1,0:T(8,128)}, u32[]{:S(2)}) copy-start(f32[128,128]{1,0:T(8,128)} %refs_6_.1) | copy-start | bytes 196612
  0.7 56.4 %copy-start.3 = (f32[128,64]{0,1:T(8,128)S(1)}, f32[128,64]{0,1:T(8,128)}, u32[]{:S(2)}) copy-start(f32[128,64]{0,1:T(8,128)} %param.14) | copy-start | bytes 98308
  0.7 56.4 %copy-start.4 = (f32[128,64]{0,1:T(8,128)S(1)}, f32[128,64]{0,1:T(8,128)}, u32[]{:S(2)}) copy-start(f32[128,64]{0,1:T(8,128)} %param.15) | copy-start | bytes 98308
  56.5 0.7 %copy-start.5 = (s32[16,16]{1,0:T(8,128)S(1)}, s32[16,16]{1,0:T(8,128)}, u32[]{:S(2)}) copy-start(s32[16,16]{1,0:T(8,128)} %refs_3_.1) | copy-start | bytes 3076

commit v5 on v4

--- a/solution.py
+++ b/solution.py
@@ -66,11 +66,11 @@
         return {"grp": lax.rem(y + ny + d, ny) * 2 + xl}
 
     x_pair = {"grp": y * 2 + 1 - xl}
-    for d in range(1, 4):
-        greet({"blk": z * 4 + lax.rem(plane + d, 4)})
     for d in (1, -1):
         greet(z_dev(d))
         greet({"blk": lax.rem(z + nz + d, nz) * 4 + x_plane})
+    for d in range(1, 4):
+        greet({"blk": z * 4 + lax.rem(plane + d, 4)})
     greet(x_pair)
     for d in range(1, ny):
         greet(y_dev(d))

time: 58.1 us -> 58 us (level)
  no operation moved by 1% of the time
where the time goes in v5:
time: 58 us; the launch traced here: 57.8 us
  Pallas kernels  55.7 us (96%)
  local copies, waits for them, and re-layouts  1.47 us (3%)
  between operations  0.65 us (1%)
    pallas_call x1, Pallas kernels, part(): call(index, occ_irrep, pair_irrep, screen, block_order, occ_irrep.reshape...  55.7 us
    unnamed x19, local copies, waits for them, and re-layouts  1.47 us

profile of v5, /device:TPU:1, one launch (start us, length us, event | category | flops | bytes accessed | tf_op | source)
XLA Modules:
  0.0 57.8 jit_solution(15720800364466404304)
XLA Ops:
  0.0 0.0 copy-start.6
  0.0 0.0 copy-start.7
  0.0 0.0 copy-start.8
  0.0 0.0 copy-start
  0.0 0.0 copy-start.1
  0.0 0.6 %copy-done.6 = s32[128]{0:T(128)S(1)} copy-done((s32[128]{0:T(128)S(1)}, s32[128]{0:T(128)}, u32[]{:S(2)}) %copy-start.6) | copy-done | bytes 536
  0.7 0.0 copy-done.7
  0.7 0.0 copy-done.8
  0.7 0.0 copy-done
  0.7 0.0 copy-start.2
  0.7 0.0 copy-start.3
  0.7 0.0 copy-start.4
  0.7 55.7 %shard_map.93 = (f32[4,128,128]{2,1,0:T(8,128)S(1)}, s32[2]{0:T(128)}) custom-call(s32[3]{0:T(128)S(1)} %copy-done, s32[128]{0:T(128)S(1)} %copy-done.6, s32[16]{0:T(128)S(1)} %copy-done.7, s32[16,16]{1,0:T(8,128)} %refs_3_.1, s32[16]{0:T(128)S(1)} %copy-done.8, s32[1,128]{1,0:T(1,128)S(1)} %bitcast.31, f32[128,128]{1,0:T(8,128)} %refs_6_.1, ...), custom_call_target="tpu_custom_call" | custom-call | tf_op jit(solution)/shard_map/pallas_call | solution.py:427
  56.4 0.0 copy-start.5
  57.0 0.0 copy-done.1
  57.0 0.0 copy-done.2
  57.0 0.0 copy-done.3
  57.1 0.0 copy-done.4
  57.1 0.1 copy-done.5
  57.1 0.7 %copy.21 = f32[4,128,128]{2,1,0:T(8,128)} copy(f32[4,128,128]{2,1,0:T(8,128)S(1)} %get-tuple-element.102) | data formatting | bytes 524288
  (1 shorter events, 0.0 us)
Async XLA Ops:
  0.0 0.7 %copy-start.6 = (s32[128]{0:T(128)S(1)}, s32[128]{0:T(128)}, u32[]{:S(2)}) copy-start(s32[128]{0:T(128)} %refs_1_.1) | copy-start | bytes 1540
  0.0 0.7 %copy-start.7 = (s32[16]{0:T(128)S(1)}, s32[16]{0:T(128)}, u32[]{:S(2)}) copy-start(s32[16]{0:T(128)} %refs_2_.1) | copy-start | bytes 196
  0.0 0.7 %copy-start.8 = (s32[16]{0:T(128)S(1)}, s32[16]{0:T(128)}, u32[]{:S(2)}) copy-start(s32[16]{0:T(128)} %refs_4_.1) | copy-start | bytes 196
  0.0 0.7 %copy-start = (s32[3]{0:T(128)S(1)}, s32[3]{0:T(128)}, u32[]{:S(2)}) copy-start(s32[3]{0:T(128)} %constant.11.clone.refs_0_) | copy-start | bytes 40
  0.0 57.0 %copy-start.1 = (f32[4,128,128]{2,1,0:T(8,128)S(1)}, f32[4,128,128]{2,1,0:T(8,128)}, u32[]{:S(2)}) copy-start(f32[4,128,128]{2,1,0:T(8,128)} %refs_7_.1) | copy-start | bytes 786436
  0.7 56.3 %copy-start.2 = (f32[128,128]{1,0:T(8,128)S(1)}, f32[128,128]{1,0:T(8,128)}, u32[]{:S(2)}) copy-start(f32[128,128]{1,0:T(8,128)} %refs_6_.1) | copy-start | bytes 196612
  0.7 56.3 %copy-start.3 = (f32[128,64]{0,1:T(8,128)S(1)}, f32[128,64]{0,1:T(8,128)}, u32[]{:S(2)}) copy-start(f32[128,64]{0,1:T(8,128)} %param.14) | copy-start | bytes 98308
  0.7 56.3 %copy-start.4 = (f32[128,64]{0,1:T(8,128)S(1)}, f32[128,64]{0,1:T(8,128)}, u32[]{:S(2)}) copy-start(f32[128,64]{0,1:T(8,128)} %param.15) | copy-start | bytes 98308
  56.4 0.7 %copy-start.5 = (s32[16,16]{1,0:T(8,128)S(1)}, s32[16,16]{1,0:T(8,128)}, u32[]{:S(2)}) copy-start(s32[16,16]{1,0:T(8,128)} %refs_3_.1) | copy-start | bytes 3076

commit v6 on v5

--- a/solution.py
+++ b/solution.py
@@ -94,61 +94,6 @@
         psub[s, :, TILE : 2 * TILE] = cyc_t[32 * s : 32 * s + 32]
     pan[z, h] = psub[h]
 
-    pl.semaphore_wait(barrier, 8 + ny - 1)
-
-    def remote(src, dst, sems, index, where):
-        return pltpu.make_async_remote_copy(
-            src_ref=src,
-            dst_ref=dst,
-            send_sem=sems.at[(0, *index)],
-            recv_sem=sems.at[(1, *index)],
-            device_id=where,
-            device_id_type=pl.DeviceIdType.MESH,
-        )
-
-    def to_x():
-        return remote(psub.at[1 - h], pan.at[z, h], sem_b, (0,), {"blk": x_dev})
-
-    def from_x():
-        return remote(psub.at[1 - h], pan.at[z, 1 - h], sem_b, (0,), {"blk": x_dev})
-
-    def to_x_z(way):
-        step = 1 - 2 * way
-        return remote(
-            psub.at[1 - h], pan.at[z, h], sem_c, (1, way, 1),
-            {"blk": lax.rem(z + nz + step, nz) * 4 + x_plane},
-        )
-
-    tiles = (h, 1 - h)
-    reach = ((nz // 2, nz - 1 - nz // 2), (nz - 1 - nz // 2, nz // 2))
-
-    def pass_z(kind, way, t):
-        step = 1 - 2 * way
-        src = lax.rem(z + nz - step * (t - 1), nz)
-        at = pan.at[src, tiles[kind]]
-        return remote(at, at, sem_c, (kind, way, t), z_dev(step))
-
-    def got_z(kind, way, t):
-        step = 1 - 2 * way
-        src = lax.rem(z + nz - step * t, nz)
-        at = pan.at[src, tiles[kind]]
-        return remote(at, at, sem_c, (kind, way, t), z_dev(step))
-
-    def start_z(kind, t):
-        for way in range(2):
-            if t <= reach[kind][way]:
-                if t > 1:
-                    got_z(kind, way, t - 1).wait_recv()
-                pass_z(kind, way, t).start()
-
-    def rows_to(src, where, k):
-        return remote(lhs.at[src], lhs.at[src], sem_a, (k,), {"blk": where})
-
-    to_x().start()
-    for way in range(2):
-        if reach[1][way]:
-            to_x_z(way).start()
-    start_z(0, 1)
     for n in (0, 1, 4, 5, 6, 7):
         fetch(n).wait()
 
@@ -198,6 +143,61 @@
         lhs[plane, rows, 0:TILE] = packed[:CAP]
         lhs[plane, rows, TILE : 2 * TILE] = packed[CAP:]
 
+    pl.semaphore_wait(barrier, 8 + ny - 1)
+
+    def remote(src, dst, sems, index, where):
+        return pltpu.make_async_remote_copy(
+            src_ref=src,
+            dst_ref=dst,
+            send_sem=sems.at[(0, *index)],
+            recv_sem=sems.at[(1, *index)],
+            device_id=where,
+            device_id_type=pl.DeviceIdType.MESH,
+        )
+
+    def to_x():
+        return remote(psub.at[1 - h], pan.at[z, h], sem_b, (0,), {"blk": x_dev})
+
+    def from_x():
+        return remote(psub.at[1 - h], pan.at[z, 1 - h], sem_b, (0,), {"blk": x_dev})
+
+    def to_x_z(way):
+        step = 1 - 2 * way
+        return remote(
+            psub.at[1 - h], pan.at[z, h], sem_c, (1, way, 1),
+            {"blk": lax.rem(z + nz + step, nz) * 4 + x_plane},
+        )
+
+    tiles = (h, 1 - h)
+    reach = ((nz // 2, nz - 1 - nz // 2), (nz - 1 - nz // 2, nz // 2))
+
+    def pass_z(kind, way, t):
+        step = 1 - 2 * way
+        src = lax.rem(z + nz - step * (t - 1), nz)
+        at = pan.at[src, tiles[kind]]
+        return remote(at, at, sem_c, (kind, way, t), z_dev(step))
+
+    def got_z(kind, way, t):
+        step = 1 - 2 * way
+        src = lax.rem(z + nz - step * t, nz)
+        at = pan.at[src, tiles[kind]]
+        return remote(at, at, sem_c, (kind, way, t), z_dev(step))
+
+    def start_z(kind, t):
+        for way in range(2):
+            if t <= reach[kind][way]:
+                if t > 1:
+                    got_z(kind, way, t - 1).wait_recv()
+                pass_z(kind, way, t).start()
+
+    def rows_to(src, where, k):
+        return remote(lhs.at[src], lhs.at[src], sem_a, (k,), {"blk": where})
+
+    to_x().start()
+    for way in range(2):
+        if reach[1][way]:
+            to_x_z(way).start()
+    start_z(0, 1)
     rows_to(plane, x_dev, 0).start()
     rows_to(plane, c_dev, 1).start()
     for kind in range(2):

time: 58 us -> 58 us (level)
  no operation moved by 1% of the time
where the time goes in v6:
time: 58 us; the launch traced here: 57.8 us
  Pallas kernels  55.7 us (96%)
  local copies, waits for them, and re-layouts  1.47 us (3%)
  between operations  0.65 us (1%)
    pallas_call x1, Pallas kernels, part(): call(index, occ_irrep, pair_irrep, screen, block_order, occ_irrep.reshape...  55.7 us
    unnamed x19, local copies, waits for them, and re-layouts  1.47 us

profile of v6, /device:TPU:1, one launch (start us, length us, event | category | flops | bytes accessed | tf_op | source)
XLA Modules:
  0.0 57.8 jit_solution(15291969381626713376)
XLA Ops:
  0.0 0.0 copy-start.6
  0.0 0.0 copy-start.7
  0.0 0.0 copy-start.8
  0.0 0.0 copy-start
  0.0 0.0 copy-start.1
  0.0 0.6 %copy-done.6 = s32[128]{0:T(128)S(1)} copy-done((s32[128]{0:T(128)S(1)}, s32[128]{0:T(128)}, u32[]{:S(2)}) %copy-start.6) | copy-done | bytes 536
  0.7 0.0 copy-done.7
  0.7 0.0 copy-done.8
  0.7 0.0 copy-done
  0.7 0.0 copy-start.2
  0.7 0.0 copy-start.3
  0.7 0.0 copy-start.4
  0.7 55.7 %shard_map.93 = (f32[4,128,128]{2,1,0:T(8,128)S(1)}, s32[2]{0:T(128)}) custom-call(s32[3]{0:T(128)S(1)} %copy-done, s32[128]{0:T(128)S(1)} %copy-done.6, s32[16]{0:T(128)S(1)} %copy-done.7, s32[16,16]{1,0:T(8,128)} %refs_3_.1, s32[16]{0:T(128)S(1)} %copy-done.8, s32[1,128]{1,0:T(1,128)S(1)} %bitcast.31, f32[128,128]{1,0:T(8,128)} %refs_6_.1, ...), custom_call_target="tpu_custom_call" | custom-call | tf_op jit(solution)/shard_map/pallas_call | solution.py:427
  56.4 0.0 copy-start.5
  57.0 0.0 copy-done.1
  57.0 0.0 copy-done.2
  57.0 0.0 copy-done.3
  57.1 0.0 copy-done.4
  57.1 0.1 copy-done.5
  57.1 0.7 %copy.21 = f32[4,128,128]{2,1,0:T(8,128)} copy(f32[4,128,128]{2,1,0:T(8,128)S(1)} %get-tuple-element.102) | data formatting | bytes 524288
  (1 shorter events, 0.0 us)
Async XLA Ops:
  0.0 0.7 %copy-start.6 = (s32[128]{0:T(128)S(1)}, s32[128]{0:T(128)}, u32[]{:S(2)}) copy-start(s32[128]{0:T(128)} %refs_1_.1) | copy-start | bytes 1540
  0.0 0.7 %copy-start.7 = (s32[16]{0:T(128)S(1)}, s32[16]{0:T(128)}, u32[]{:S(2)}) copy-start(s32[16]{0:T(128)} %refs_2_.1) | copy-start | bytes 196
  0.0 0.7 %copy-start.8 = (s32[16]{0:T(128)S(1)}, s32[16]{0:T(128)}, u32[]{:S(2)}) copy-start(s32[16]{0:T(128)} %refs_4_.1) | copy-start | bytes 196
  0.0 0.7 %copy-start = (s32[3]{0:T(128)S(1)}, s32[3]{0:T(128)}, u32[]{:S(2)}) copy-start(s32[3]{0:T(128)} %constant.11.clone.refs_0_) | copy-start | bytes 40
  0.0 57.0 %copy-start.1 = (f32[4,128,128]{2,1,0:T(8,128)S(1)}, f32[4,128,128]{2,1,0:T(8,128)}, u32[]{:S(2)}) copy-start(f32[4,128,128]{2,1,0:T(8,128)} %refs_7_.1) | copy-start | bytes 786436
  0.7 56.3 %copy-start.2 = (f32[128,128]{1,0:T(8,128)S(1)}, f32[128,128]{1,0:T(8,128)}, u32[]{:S(2)}) copy-start(f32[128,128]{1,0:T(8,128)} %refs_6_.1) | copy-start | bytes 196612
  0.7 56.3 %copy-start.3 = (f32[128,64]{0,1:T(8,128)S(1)}, f32[128,64]{0,1:T(8,128)}, u32[]{:S(2)}) copy-start(f32[128,64]{0,1:T(8,128)} %param.14) | copy-start | bytes 98308
  0.7 56.3 %copy-start.4 = (f32[128,64]{0,1:T(8,128)S(1)}, f32[128,64]{0,1:T(8,128)}, u32[]{:S(2)}) copy-start(f32[128,64]{0,1:T(8,128)} %param.15) | copy-start | bytes 98308
  56.4 0.7 %copy-start.5 = (s32[16,16]{1,0:T(8,128)S(1)}, s32[16,16]{1,0:T(8,128)}, u32[]{:S(2)}) copy-start(s32[16,16]{1,0:T(8,128)} %refs_3_.1) | copy-start | bytes 3076
